TPU v7x, 512 devices: a whole 4x8x8 slice. The times are simulated.
512 devices in a mesh: ctx: 16 (over y_hi, x), set: 32 (over z, y_lo, core).
Axes of the slice: x: 4, y: 8 (y_hi: 4, y_lo: 2; y = y_hi * 2 + y_lo), z: 8, core: 2. Of those that a mesh axis runs over, the one named last changes fastest.
Arguments:
- queries: bfloat16 [32, 256, 2048], P('set', 'ctx'), may hold values from -160 to 160
- out_grad: bfloat16 [32, 256, 2048], P('set', 'ctx'), may hold values from -24 to 24
- branch_kv: bfloat16 [32, 256, 256], P('set', 'ctx'), may hold values from -10.75 to 10.75
- trunk_kv: bfloat16 [8192, 256], P('ctx'), may hold values from -6 to 6
- parent: int32 [32, 256], P('set'), may hold values from -1 to 254, as said below
- prefix: int32 [32, 256], P('set'), may hold values from 2048 to 8192, as said below
Outputs:
- query_grad: bfloat16 [32, 256, 2048], P('set', 'ctx')
- branch_grad: float32 [32, 256, 256], P('set', 'ctx')
- trunk_grad: float32 [8192, 256], P(('ctx', 'set'))
Inputs may be any that keep to these rules, and one draw needn't show every extreme that they name: parent[s, r] is -1 for r a multiple of 64, else between max(r - 32, 0) and r - 1; the last row's parent is row 254. `prefix`: row 0 of every set sees the whole trunk.
All inputs are finite; a program needn't handle non-finite values.
Results may differ from a plain program's by a relative error of at most 0.005.
Values may be sent and summed in bfloat16 or wider, within the bound.
No kernel may reach another device: no remote copies, remote signals or barrier semaphores. Data moves between devices by JAX's collectives and lax.ppermute only.
A program may use at most 64 MiB of HBM per device.

v0:
```python
import jax
import jax.numpy as jnp
from jax import lax
from jax.experimental import pallas as pl
from jax.experimental.pallas import tpu as pltpu
from jax.sharding import Mesh, PartitionSpec as P


MASKED = -1e30
TILE = 16
SET = ("z", "yl", "c")


def ancestors_t(parent_row):
    count = parent_row.shape[0]
    labels = jnp.arange(count, dtype=jnp.int32)
    links = (parent_row[None, :] == labels[:, None]) | (labels[:, None] == labels[None, :])
    reach = links.astype(jnp.bfloat16)
    for _ in range(max(count - 1, 1).bit_length()):
        reach = jnp.minimum(jnp.dot(reach, reach, preferred_element_type=jnp.float32), 1.0).astype(
            jnp.bfloat16
        )
    return reach


def dot_nt(left, right):
    return lax.dot_general(
        left, right, (((1,), (1,)), ((), ())), preferred_element_type=jnp.float32
    )


def dot_tn(left, right):
    return lax.dot_general(
        left, right, (((0,), (0,)), ((), ())), preferred_element_type=jnp.float32
    )


def stack_heads(src, which, dst):
    groups, _, own, _ = src.shape
    width = dst.shape[1]
    rows = groups * own
    for h in range(dst.shape[0] // rows):
        for y in range(groups):
            dst[pl.ds(h * rows + y * own, own), :] = src[y, which, :, pl.ds(h * width, width)]


def source(pos_ref, k, blocks):
    return lax.rem(pos_ref[0] + blocks - k, blocks)


def stats_kernel(pos_ref, lim_ref, reach_ref, qg_ref, *refs):
    blocks = 4
    kvs = refs[:blocks]
    out_ref, tops_ref, e_ref, s_ref, qs, gs = refs[blocks:]
    keys, wide = kvs[0].shape
    width = wide // 2
    lanes = qs.shape[0]
    scale = width ** (-0.5)
    trunk = keys - TILE
    stack_heads(qg_ref, 0, qs)
    stack_heads(qg_ref, 1, gs)
    ids = lax.broadcasted_iota(jnp.int32, (TILE, lanes), 0)
    room = jnp.broadcast_to(lim_ref[...], (TILE, lanes)) - ids
    top = jnp.full((1, lanes), MASKED, jnp.float32)
    total = jnp.zeros((1, lanes), jnp.float32)
    slope = jnp.zeros((1, lanes), jnp.float32)
    for k in range(blocks):
        b = source(pos_ref, k, blocks)
        e_ref[k] = dot_nt(kvs[k][:, :width], qs[...])
        s_ref[k] = dot_nt(kvs[k][:, width:], gs[...])

        def mask(t, best):
            at = pl.ds(pl.multiple_of(t * TILE, TILE), TILE)
            s = jnp.where(room > b * trunk + t * TILE, e_ref[k, at, :] * scale, MASKED)
            e_ref[k, at, :] = s
            return jnp.maximum(best, s)

        best = lax.fori_loop(
            0, trunk // TILE, mask, jnp.full((TILE, lanes), MASKED, jnp.float32), unroll=2
        )
        tree = jnp.where(
            reach_ref[pl.ds(pl.multiple_of(b * TILE, TILE), TILE), :] > 0.5,
            e_ref[k, pl.ds(trunk, TILE), :] * scale,
            MASKED,
        )
        e_ref[k, pl.ds(trunk, TILE), :] = tree
        best = jnp.max(jnp.maximum(best, tree), axis=0, keepdims=True)
        now = jnp.maximum(top, best)
        fade = jnp.exp(top - now)
        tops_ref[pl.ds(k, 1), :] = now

        def add(t, sums):
            at = pl.ds(pl.multiple_of(t * TILE, TILE), TILE)
            p = jnp.exp(e_ref[k, at, :] - now)
            e_ref[k, at, :] = p
            return (sums[0] + p, sums[1] + p * s_ref[k, at, :])

        zero = jnp.zeros((TILE, lanes), jnp.float32)
        l, d = lax.fori_loop(0, keys // TILE, add, (zero, zero), unroll=3)
        total = total * fade + jnp.sum(l, axis=0, keepdims=True)
        slope = slope * fade + jnp.sum(d, axis=0, keepdims=True)
        top = now
    out_ref[0:1, :] = top + jnp.log(total)
    out_ref[1:2, :] = slope / total


def grads_kernel(pos_ref, stats_ref, tops_ref, e_ref, s_ref, qs, gs, *refs):
    blocks, keys, lanes = e_ref.shape
    kvs = refs[:blocks]
    qkeep_ref, qsend_ref, keep_ref, send_ref, tkeep_ref, tsend_ref = refs[blocks : blocks + 6]
    d_scr, p_scr, kv_scr, dq_scr, q_scr, tree_scr = refs[blocks + 6 :]
    groups = stats_ref.shape[0]
    own = qkeep_ref.shape[1]
    rows = groups * own
    width = qs.shape[1]
    scale = width ** (-0.5)
    trunk = keys - TILE
    mine = pos_ref[1]
    q_half = lax.div(pos_ref[2], 2)
    tree_half = lax.div(pos_ref[0], 2)
    parts = [stats_ref[i, 0:1, :] for i in range(groups)]
    top = parts[0]
    for part in parts[1:]:
        top = jnp.maximum(top, part)
    total = jnp.zeros_like(top)
    for part in parts:
        total = total + jnp.exp(part - top)
    log_total = top + jnp.log(total)
    delta = jnp.zeros_like(top)
    for i in range(groups):
        delta = delta + jnp.exp(parts[i] - log_total) * stats_ref[i, 1:2, :]
    for k in range(blocks):
        b = source(pos_ref, k, blocks)
        fade = jnp.exp(tops_ref[pl.ds(k, 1), :] - log_total)

        def tile(t, carry):
            at = pl.ds(pl.multiple_of(t * TILE, TILE), TILE)
            p = e_ref[k, at, :] * fade
            d_scr[at, :] = (p * (s_ref[k, at, :] - delta)).astype(jnp.bfloat16)
            p_scr[at, :] = p.astype(jnp.bfloat16)
            return carry

        lax.fori_loop(0, keys // TILE, tile, 0, unroll=3)
        dk = scale * jnp.dot(d_scr[...], qs[...], preferred_element_type=jnp.float32)
        dv = jnp.dot(p_scr[...], gs[...], preferred_element_type=jnp.float32)
        kv_scr[:, :, :, :width] = dk[:trunk].reshape(trunk // (2 * TILE), 2, TILE, width)
        kv_scr[:, :, :, width:] = dv[:trunk].reshape(trunk // (2 * TILE), 2, TILE, width)
        tree_scr[b, :, :width] = dk[trunk:]
        tree_scr[b, :, width:] = dv[trunk:]
        keep_ref[b] = kv_scr[:, mine]
        send_ref[b] = kv_scr[:, 1 - mine].astype(jnp.bfloat16)
        part = dot_tn(kvs[k][:, :width], d_scr[...])
        if k == 0:
            dq_scr[...] = part
        else:
            dq_scr[...] += part
    for h in range(lanes // rows):
        piece = (scale * dq_scr[:, pl.ds(h * rows, rows)]).T
        q_scr[:, :, pl.ds(h * width, width)] = piece.reshape(groups, own, width)
    qkeep_ref[...] = q_scr[pl.ds(2 * q_half, 2)]
    qsend_ref[...] = q_scr[pl.ds(2 - 2 * q_half, 2)].astype(jnp.bfloat16)
    tkeep_ref[...] = tree_scr[pl.ds(2 * tree_half, 2)]
    tsend_ref[...] = tree_scr[pl.ds(2 - 2 * tree_half, 2)]


def swap(x, axis):
    return lax.all_to_all(x, axis, 0, 0)


def spread(x, axis):
    return swap(jnp.broadcast_to(x[None], (lax.axis_size(axis),) + x.shape), axis)


def turn(x, axis, k):
    n = lax.axis_size(axis)
    return lax.ppermute(x, axis, [(i, (i + k) % n) for i in range(n)])


def meet(x, axis, bit):
    return lax.ppermute(x, axis, [(i, i ^ bit) for i in range(lax.axis_size(axis))])


def pick(x, which):
    return lax.dynamic_index_in_dim(x, which, 0, keepdims=False)


def per_device(queries, out_grad, branch_kv, trunk_kv, parent, prefix):
    bf16, f32 = jnp.bfloat16, jnp.float32
    width = trunk_kv.shape[1] // 2
    own = queries.shape[1]
    heads = queries.shape[2] // width
    nx, ny = lax.axis_size("x"), lax.axis_size("yh")
    x, yh, core = lax.axis_index("x"), lax.axis_index("yh"), lax.axis_index("c")
    span = trunk_kv.shape[0] * nx
    rows = own * ny
    lanes = rows * heads
    pos = jnp.stack([x, core, yh])

    qg = spread(jnp.stack([queries[0], out_grad[0]]), "yh")
    kv = jnp.concatenate([trunk_kv, branch_kv[0]], axis=0)
    kvs = [kv] + [turn(kv, "x", k) for k in range(1, nx)]

    mine = prefix[0].reshape(ny, nx, own)[:, x].reshape(rows)
    lim = jnp.tile(mine - yh * span, heads)[None]
    reach = ancestors_t(parent[0])
    reach = lax.dynamic_slice_in_dim(reach, yh * nx * own, nx * own, 0)
    reach = reach.reshape(nx * own, ny, nx, own)[:, :, x].reshape(nx * own, rows)
    reach = jnp.tile(reach.astype(f32), (1, heads))

    keys = kv.shape[0]
    vmem = pl.BlockSpec(memory_space=pltpu.VMEM)
    smem = pl.BlockSpec(memory_space=pltpu.SMEM)
    shape = jax.ShapeDtypeStruct
    stats, tops, e, s, qs, gs = pl.pallas_call(
        stats_kernel,
        out_shape=(
            shape((2, lanes), f32),
            shape((nx, lanes), f32),
            shape((nx, keys, lanes), f32),
            shape((nx, keys, lanes), f32),
            shape((lanes, width), bf16),
            shape((lanes, width), bf16),
        ),
        in_specs=[smem] + [vmem] * (3 + nx),
        out_specs=(vmem,) * 6,
        compiler_params=pltpu.CompilerParams(vmem_limit_bytes=6 << 20),
        name="stats",
    )(pos, lim, reach, qg, *kvs)
    stats = spread(stats, "yh")
    pieces = trunk_kv.shape[0] // (2 * own)
    q_keep, q_send, keep, send, t_keep, t_send = pl.pallas_call(
        grads_kernel,
        out_shape=(
            shape((ny // 2, own, heads * width), f32),
            shape((ny // 2, own, heads * width), bf16),
            shape((nx, pieces, own, 2 * width), f32),
            shape((nx, pieces, own, 2 * width), bf16),
            shape((nx // 2, own, 2 * width), f32),
            shape((nx // 2, own, 2 * width), f32),
        ),
        in_specs=[smem] + [vmem] * (6 + nx),
        out_specs=(vmem,) * 6,
        scratch_shapes=[
            pltpu.VMEM((keys, lanes), bf16),
            pltpu.VMEM((keys, lanes), bf16),
            pltpu.VMEM((pieces, 2, own, 2 * width), f32),
            pltpu.VMEM((width, lanes), f32),
            pltpu.VMEM((ny, own, heads * width), f32),
            pltpu.VMEM((nx, own, 2 * width), f32),
        ],
        compiler_params=pltpu.CompilerParams(vmem_limit_bytes=10 << 20),
        name="grads",
    )(pos, stats, tops, e, s, qs, gs, *kvs)
    other = turn(send, "c", 1)
    trunk = (keep + other.astype(f32)).astype(bf16).reshape(nx * pieces, own, 2 * width)
    trunk = swap(trunk, ("x", "z", "yl"))
    low = lax.rem(yh, 2)
    part = q_keep + meet(q_send, "yh", 2).astype(f32)
    query_grad = pick(part, low) + meet(pick(part, 1 - low).astype(bf16), "yh", 1).astype(f32)
    query_grad = query_grad.astype(bf16)
    low = lax.rem(x, 2)
    part = t_keep + meet(t_send, "x", 2)
    branch = pick(part, low) + meet(pick(part, 1 - low), "x", 1)
    trunk = jnp.sum(trunk.astype(f32), axis=0)
    return (query_grad[None], branch[None], trunk)


def solution(mesh):
    fine = Mesh(mesh.devices.reshape(4, 4, 8, 2, 2), ("yh", "x") + SET)
    ctx = ("yh", "x")
    return jax.shard_map(
        per_device,
        mesh=fine,
        in_specs=(
            P(SET, ctx, None),
            P(SET, ctx, None),
            P(SET, ctx, None),
            P(ctx, None),
            P(SET, None),
            P(SET, None),
        ),
        out_specs=(P(SET, ctx, None), P(SET, ctx, None), P(ctx + SET, None)),
        check_vma=False,
    )
```

profile of v0, /device:TPU:40, one launch (start us, length us, event | category | flops | bytes accessed | tf_op | source)
XLA Modules:
  0.0 105.4 jit_solution(13536271935085395435)
XLA Ops:
  0.6 1.0 pad_maximum_fusion.refs_0_
  1.6 3.4 %collective-permute-start = (bf16[528,256]{1,0:T(8,128)(2,1)S(1)}, bf16[528,256]{1,0:T(8,128)(2,1)S(1)}, u32[]{:S(2)}, u32[]{:S(2)}) collective-permute-start(bf16[528,256]{1,0:T(8,128)(2,1)S(1)} %pad_maximum_fusion.refs_0_), channel_id=1, source_target_pairs={{0,32},{32,64},{64,96},{96,0},{1,33},{33,65},{65,97},{97,1},{2,34}... | collective-permute-start | bytes 811016 | tf_op jit(solution)/shard_map/ppermute | solution.py:176
  5.0 4.6 %collective-permute-start.1 = (bf16[528,256]{1,0:T(8,128)(2,1)S(1)}, bf16[528,256]{1,0:T(8,128)(2,1)S(1)}, u32[]{:S(2)}, u32[]{:S(2)}) collective-permute-start(bf16[528,256]{1,0:T(8,128)(2,1)S(1)} %pad_maximum_fusion.refs_0_), channel_id=1, source_target_pairs={{0,64},{32,96},{64,0},{96,32},{1,65},{33,97},{65,1},{97,33},{2,66}... | collective-permute-start | bytes 811016 | tf_op jit(solution)/shard_map/ppermute | solution.py:176
  9.7 3.3 %collective-permute-start.2 = (bf16[528,256]{1,0:T(8,128)(2,1)S(1)}, bf16[528,256]{1,0:T(8,128)(2,1)S(1)}, u32[]{:S(2)}, u32[]{:S(2)}) collective-permute-start(bf16[528,256]{1,0:T(8,128)(2,1)S(1)} %pad_maximum_fusion.refs_0_), channel_id=1, source_target_pairs={{0,96},{32,0},{64,32},{96,64},{1,97},{33,1},{65,33},{97,65},{2,98}... | collective-permute-start | bytes 811016 | tf_op jit(solution)/shard_map/ppermute | solution.py:176
  13.0 0.9 pad_maximum_fusion.1
  13.9 0.9 broadcast_in_dim.8
  14.8 7.2 %all-to-all-start = ((bf16[4,2,16,2048]{3,2,1,0:T(8,128)(2,1)}), bf16[4,2,16,2048]{3,2,1,0:T(8,128)(2,1)S(1)}, u32[]{:S(2)}, u32[]{:S(2)}) async-start(bf16[4,2,16,2048]{3,2,1,0:T(8,128)(2,1)} %broadcast_in_dim.8), calls=%async_computation | async-start | bytes 1048576 | tf_op jit(solution)/shard_map/all_to_all | solution.py:167
  22.0 1.3 %fusion.1 = bf16[256,256]{1,0:T(8,128)(2,1)S(1)} fusion(s32[256]{0:T(256)} %bitcast.40), kind=kOutput, calls=%fused_computation.8 | convolution fusion | flops 67567616 | bytes 132096 | tf_op jit(solution)/shard_map/dot_general | solution.py:20
  23.3 0.4 fusion.3
  23.7 0.4 fusion.5
  24.2 0.4 fusion.7
  24.7 0.1 copy.11
  24.8 0.1 copy.12
  25.0 0.2 tile.8.reach_ref
  25.1 0.5 broadcast.37
  25.6 1.3 %reduce.3 = s32[256]{0:T(256)S(1)} reduce(s32[1,256]{1,0:T(1,128)} %param.11, s32[]{:T(128)} %broadcast.37), dimensions={0}, to_apply=%param.11.reduce_sub_computation.3 | reduce | bytes 2052 | tf_op args[5]
  27.0 0.1 reshape_squeeze.2
  27.1 0.1 sub.21
  27.2 0.1 broadcast_in_dim_tile.3.lim_ref
  27.3 0.1 pad_add_fusion.pos_ref
  27.3 0.0 collective-permute-done.refs_1_
  27.3 0.0 collective-permute-done.1.refs_2_
  27.3 0.0 collective-permute-done.2.refs_3_
  27.4 5.9 %all-to-all-done.qg_ref = bf16[4,2,16,2048]{3,2,1,0:T(8,128)(2,1)S(1)} async-done(((bf16[4,2,16,2048]{3,2,1,0:T(8,128)(2,1)}), bf16[4,2,16,2048]{3,2,1,0:T(8,128)(2,1)S(1)}, u32[]{:S(2)}, u32[]{:S(2)}) %all-to-all-start) | async-done | bytes 524320 | tf_op jit(solution)/shard_map/all_to_all | solution.py:167
  33.3 8.8 %stats.1 = (f32[2,1024]{1,0:T(2,128)S(1)}, f32[4,1024]{1,0:T(4,128)S(1)}, f32[4,528,1024]{2,1,0:T(8,128)S(1)}, f32[4,528,1024]{2,1,0:T(8,128)S(1)}, bf16[1024,12...) custom-call(s32[3]{0:T(128)S(1)} %pad_add_fusion.pos_ref, s32[1,1024]{1,0:T(1,128)S(1)} %broadcast_in_dim_tile.3.lim_ref, ...), custom_call_target="tpu_custom_call" | custom-call | tf_op jit(solution)/shard_map/stats/pallas_call | solution.py:214
  42.1 9.4 %all_to_all.15.stats_ref = f32[4,2,1024]{2,1,0:T(2,128)S(1)} all-to-all(f32[4,2,1024]{2,1,0:T(2,128)S(1)} %broadcast_in_dim.9), channel_id=1, replica_groups=mesh['yh'=4,'x'=4,'z'=8,'yl'=2,'c'=2] {'yh'}, dimensions={0} | all-to-all | bytes 65536 | tf_op jit(solution)/shard_map/all_to_all | solution.py:167
  51.5 6.2 %grads.1 = (f32[2,16,2048]{2,1,0:T(8,128)S(1)}, bf16[2,16,2048]{2,1,0:T(8,128)(2,1)S(1)}, f32[4,16,16,256]{3,2,1,0:T(8,128)S(1)}, bf16[4,16,16,256]{3,2,1,0:T(8,...) custom-call(s32[3]{0:T(128)S(1)} %pad_add_fusion.pos_ref, f32[4,2,1024]{2,1,0:T(2,128)S(1)} %all_to_all.15.stats_ref, ...), custom_call_target="tpu_custom_call" | custom-call | tf_op jit(solution)/shard_map/grads/pallas_call | solution.py:231
  57.7 1.9 %collective-permute-start.7 = (bf16[4,16,16,256]{3,2,1,0:T(8,128)(2,1)S(1)}, bf16[4,16,16,256]{3,2,1,0:T(8,128)(2,1)S(1)}, u32[]{:S(2)}, u32[]{:S(2)}) collective-permute-start(bf16[4,16,16,256]{3,2,1,0:T(8,128)(2,1)S(1)} %get-tuple-element.26), channel_id=1, source_target_pairs={{0,1},{1,0},{2,3},{3,2},{4,5},{5,4},{6,7},{7,6},{8,9},{9,8},{10,11... | collective-permute-start | bytes 1572872 | tf_op jit(solution)/shard_map/ppermute | solution.py:176
  59.6 2.5 %collective-permute-start.5 = (f32[2,16,256]{2,1,0:T(8,128)S(1)}, f32[2,16,256]{2,1,0:T(8,128)S(1)}, u32[]{:S(2)}, u32[]{:S(2)}) collective-permute-start(f32[2,16,256]{2,1,0:T(8,128)S(1)} %get-tuple-element.24), channel_id=1, source_target_pairs={{0,64},{32,96},{64,0},{96,32},{1,65},{33,97},{65,1},{97,33},{2,66}... | collective-permute-start | bytes 98312 | tf_op jit(solution)/shard_map/ppermute | solution.py:180
  62.1 7.4 %collective-permute-start.3 = (bf16[2,16,2048]{2,1,0:T(8,128)(2,1)S(1)}, bf16[2,16,2048]{2,1,0:T(8,128)(2,1)S(1)}, u32[]{:S(2)}, u32[]{:S(2)}) collective-permute-start(bf16[2,16,2048]{2,1,0:T(8,128)(2,1)S(1)} %get-tuple-element.22), channel_id=1, source_target_pairs={{0,256},{128,384},{256,0},{384,128},{1,257},{129,385},{257,1},{385... | collective-permute-start | bytes 393224 | tf_op jit(solution)/shard_map/ppermute | solution.py:180
  69.5 0.0 collective-permute-done.5
  69.5 2.5 %collective-permute-start.6 = (f32[16,256]{1,0:T(8,128)S(1)}, f32[16,256]{1,0:T(8,128)S(1)}, u32[]{:S(2)}, u32[]{:S(2)}) collective-permute-start(f32[16,256]{1,0:T(8,128)S(1)} %dynamic-slice_bitcast_fusion), channel_id=1, source_target_pairs={{0,32},{32,0},{64,96},{96,64},{1,33},{33,1},{65,97},{97,65},{2,34}... | collective-permute-start | bytes 49160 | tf_op jit(solution)/shard_map/ppermute | solution.py:180
  72.0 0.0 collective-permute-done.7
  72.0 1.0 add_convert_fusion
  73.0 15.3 %all-to-all-start.2 = ((bf16[64,16,256]{2,1,0:T(8,128)(2,1)}), bf16[64,16,256]{2,1,0:T(8,128)(2,1)S(1)}, u32[]{:S(2)}, u32[]{:S(2)}) async-start(bf16[64,16,256]{2,1,0:T(8,128)(2,1)} %bitcast.13), calls=%async_computation.2 | async-start | bytes 1048576 | tf_op jit(solution)/shard_map/all_to_all | solution.py:167
  88.4 0.0 collective-permute-done.3
  88.4 2.5 %collective-permute-start.4 = (bf16[16,2048]{1,0:T(8,128)(2,1)S(1)}, bf16[16,2048]{1,0:T(8,128)(2,1)S(1)}, u32[]{:S(2)}, u32[]{:S(2)}) collective-permute-start(bf16[16,2048]{1,0:T(8,128)(2,1)S(1)} %fusion.18), channel_id=1, source_target_pairs={{0,128},{128,0},{256,384},{384,256},{1,129},{129,1},{257,385},{385... | collective-permute-start | bytes 196616 | tf_op jit(solution)/shard_map/ppermute | solution.py:180
  91.0 0.0 collective-permute-done.6
  91.0 0.6 fusion.21
  91.6 4.2 %collective-permute-done.4 = bf16[16,2048]{1,0:T(8,128)(2,1)S(1)} collective-permute-done((bf16[16,2048]{1,0:T(8,128)(2,1)S(1)}, bf16[16,2048]{1,0:T(8,128)(2,1)S(1)}, u32[]{:S(2)}, u32[]{:S(2)}) %collective-permute-start.4) | collective-permute-done | bytes 65568 | tf_op jit(solution)/shard_map/ppermute | solution.py:180
  95.8 0.6 fusion.19
  96.5 8.2 %all-to-all-done.2 = bf16[64,16,256]{2,1,0:T(8,128)(2,1)S(1)} async-done(((bf16[64,16,256]{2,1,0:T(8,128)(2,1)}), bf16[64,16,256]{2,1,0:T(8,128)(2,1)S(1)}, u32[]{:S(2)}, u32[]{:S(2)}) %all-to-all-start.2) | async-done | bytes 524320 | tf_op jit(solution)/shard_map/all_to_all | solution.py:167
  104.7 0.7 convert_reduce_fusion
  (12 shorter events, 0.2 us)
Async XLA Ops:
  1.6 25.7 %collective-permute-start = (bf16[528,256]{1,0:T(8,128)(2,1)S(1)}, bf16[528,256]{1,0:T(8,128)(2,1)S(1)}, u32[]{:S(2)}, u32[]{:S(2)}) collective-permute-start(bf16[528,256]{1,0:T(8,128)(2,1)S(1)} %pad_maximum_fusion.refs_0_), channel_id=1, source_target_pairs={{0,32},{32,64},{64,96},{96,0},{1,33},{33,65},{65,97},{97,1},{2,34}... | collective-permute-start | bytes 811016 | tf_op jit(solution)/shard_map/ppermute | solution.py:176
  5.0 22.3 %collective-permute-start.1 = (bf16[528,256]{1,0:T(8,128)(2,1)S(1)}, bf16[528,256]{1,0:T(8,128)(2,1)S(1)}, u32[]{:S(2)}, u32[]{:S(2)}) collective-permute-start(bf16[528,256]{1,0:T(8,128)(2,1)S(1)} %pad_maximum_fusion.refs_0_), channel_id=1, source_target_pairs={{0,64},{32,96},{64,0},{96,32},{1,65},{33,97},{65,1},{97,33},{2,66}... | collective-permute-start | bytes 811016 | tf_op jit(solution)/shard_map/ppermute | solution.py:176
  9.7 17.7 %collective-permute-start.2 = (bf16[528,256]{1,0:T(8,128)(2,1)S(1)}, bf16[528,256]{1,0:T(8,128)(2,1)S(1)}, u32[]{:S(2)}, u32[]{:S(2)}) collective-permute-start(bf16[528,256]{1,0:T(8,128)(2,1)S(1)} %pad_maximum_fusion.refs_0_), channel_id=1, source_target_pairs={{0,96},{32,0},{64,32},{96,64},{1,97},{33,1},{65,33},{97,65},{2,98}... | collective-permute-start | bytes 811016 | tf_op jit(solution)/shard_map/ppermute | solution.py:176
  14.8 18.5 %all-to-all-start = ((bf16[4,2,16,2048]{3,2,1,0:T(8,128)(2,1)}), bf16[4,2,16,2048]{3,2,1,0:T(8,128)(2,1)S(1)}, u32[]{:S(2)}, u32[]{:S(2)}) async-start(bf16[4,2,16,2048]{3,2,1,0:T(8,128)(2,1)} %broadcast_in_dim.8), calls=%async_computation | async-start | bytes 1048576 | tf_op jit(solution)/shard_map/all_to_all | solution.py:167
  57.7 14.4 %collective-permute-start.7 = (bf16[4,16,16,256]{3,2,1,0:T(8,128)(2,1)S(1)}, bf16[4,16,16,256]{3,2,1,0:T(8,128)(2,1)S(1)}, u32[]{:S(2)}, u32[]{:S(2)}) collective-permute-start(bf16[4,16,16,256]{3,2,1,0:T(8,128)(2,1)S(1)} %get-tuple-element.26), channel_id=1, source_target_pairs={{0,1},{1,0},{2,3},{3,2},{4,5},{5,4},{6,7},{7,6},{8,9},{9,8},{10,11... | collective-permute-start | bytes 1572872 | tf_op jit(solution)/shard_map/ppermute | solution.py:176
  59.6 9.9 %collective-permute-start.5 = (f32[2,16,256]{2,1,0:T(8,128)S(1)}, f32[2,16,256]{2,1,0:T(8,128)S(1)}, u32[]{:S(2)}, u32[]{:S(2)}) collective-permute-start(f32[2,16,256]{2,1,0:T(8,128)S(1)} %get-tuple-element.24), channel_id=1, source_target_pairs={{0,64},{32,96},{64,0},{96,32},{1,65},{33,97},{65,1},{97,33},{2,66}... | collective-permute-start | bytes 98312 | tf_op jit(solution)/shard_map/ppermute | solution.py:180
  62.1 26.3 %collective-permute-start.3 = (bf16[2,16,2048]{2,1,0:T(8,128)(2,1)S(1)}, bf16[2,16,2048]{2,1,0:T(8,128)(2,1)S(1)}, u32[]{:S(2)}, u32[]{:S(2)}) collective-permute-start(bf16[2,16,2048]{2,1,0:T(8,128)(2,1)S(1)} %get-tuple-element.22), channel_id=1, source_target_pairs={{0,256},{128,384},{256,0},{384,128},{1,257},{129,385},{257,1},{385... | collective-permute-start | bytes 393224 | tf_op jit(solution)/shard_map/ppermute | solution.py:180
  69.5 21.5 %collective-permute-start.6 = (f32[16,256]{1,0:T(8,128)S(1)}, f32[16,256]{1,0:T(8,128)S(1)}, u32[]{:S(2)}, u32[]{:S(2)}) collective-permute-start(f32[16,256]{1,0:T(8,128)S(1)} %dynamic-slice_bitcast_fusion), channel_id=1, source_target_pairs={{0,32},{32,0},{64,96},{96,64},{1,33},{33,1},{65,97},{97,65},{2,34}... | collective-permute-start | bytes 49160 | tf_op jit(solution)/shard_map/ppermute | solution.py:180
  73.0 31.7 %all-to-all-start.2 = ((bf16[64,16,256]{2,1,0:T(8,128)(2,1)}), bf16[64,16,256]{2,1,0:T(8,128)(2,1)S(1)}, u32[]{:S(2)}, u32[]{:S(2)}) async-start(bf16[64,16,256]{2,1,0:T(8,128)(2,1)} %bitcast.13), calls=%async_computation.2 | async-start | bytes 1048576 | tf_op jit(solution)/shard_map/all_to_all | solution.py:167
  88.4 7.4 %collective-permute-start.4 = (bf16[16,2048]{1,0:T(8,128)(2,1)S(1)}, bf16[16,2048]{1,0:T(8,128)(2,1)S(1)}, u32[]{:S(2)}, u32[]{:S(2)}) collective-permute-start(bf16[16,2048]{1,0:T(8,128)(2,1)S(1)} %fusion.18), channel_id=1, source_target_pairs={{0,128},{128,0},{256,384},{384,256},{1,129},{129,1},{257,385},{385... | collective-permute-start | bytes 196616 | tf_op jit(solution)/shard_map/ppermute | solution.py:180
where the time goes:
time: 106 us; the launch traced here: 105 us
  starting transfers between devices  50.7 us (48%)
  waiting for transfers between devices  18.4 us (17%)
  Pallas kernels  15 us (14%)
  blocking collectives  9.4 us (9%)
  other arithmetic  6.31 us (6%)
  matrix products  2.65 us (2%)
  local copies, waits for them, and re-layouts  2.08 us (2%)
    all_to_all x2, starting transfers between devices, swap(): return lax.all_to_all(x, axis, 0, 0)  22.5 us
    ppermute x4, starting transfers between devices, meet(): lax.ppermute(x, axis, [(i, i ^ bit) for i in range(lax.axis_size(axis))])  14.9 us
    all_to_all x2, waiting for transfers between devices, swap(): return lax.all_to_all(x, axis, 0, 0)  14.1 us
    ppermute x4, starting transfers between devices, turn(): return lax.ppermute(x, axis, [(i, (i + k) % n) for i in range(n)])  13.3 us
    all_to_all x1, blocking collectives, swap(): return lax.all_to_all(x, axis, 0, 0)  9.4 us
    pallas_call x1, Pallas kernels, per_device(): pl.pallas_call(stats_kernel, out_shape=(shape((2, lanes), f32), shape((nx...  8.78 us
    pallas_call x1, Pallas kernels, per_device(): pl.pallas_call(grads_kernel, out_shape=(shape((ny // 2, own, heads * widt...  6.18 us
    ppermute x4, waiting for transfers between devices, meet(): lax.ppermute(x, axis, [(i, i ^ bit) for i in range(lax.axis_size(axis))])  4.2 us
  transfers between devices with their start and end apart: 10, of which 3 were waited for; matrix products, arithmetic and copies ran while one was open for 9% of the time, Pallas kernels for 0%

commit v1 on v0

--- a/solution.py
+++ b/solution.py
@@ -1,3 +1,5 @@
+import functools
+
 import jax
 import jax.numpy as jnp
 from jax import lax
@@ -48,31 +50,55 @@
     return lax.rem(pos_ref[0] + blocks - k, blocks)
 
 
-def stats_kernel(pos_ref, lim_ref, reach_ref, qg_ref, *refs):
-    blocks = 4
-    kvs = refs[:blocks]
-    out_ref, tops_ref, e_ref, s_ref, qs, gs = refs[blocks:]
+def pack_kernel(q_ref, g_ref, trunk_ref, branch_ref, qg_ref, kv_ref, sems):
+    copies = [
+        pltpu.make_async_copy(part.at[0], qg_ref.at[y, i], sems.at[y, i])
+        for y in range(qg_ref.shape[0])
+        for i, part in enumerate((q_ref, g_ref))
+    ]
+    for copy in copies:
+        copy.start()
+    trunk = trunk_ref.shape[0]
+    kv_ref[:trunk, :] = trunk_ref[...]
+    kv_ref[trunk:, :] = branch_ref[0]
+    for copy in copies:
+        copy.wait()
+
+
+def stats_kernel(shifts, last, pos_ref, lim_ref, reach_ref, *refs):
+    count = len(shifts)
+    if last:
+        qs, gs, before_ref = refs[:3]
+        kvs = refs[3 : 3 + count]
+        after_ref, tops_ref, e_ref, s_ref = refs[3 + count :]
+    else:
+        qg_ref = refs[0]
+        kvs = refs[1 : 1 + count]
+        after_ref, tops_ref, e_ref, s_ref, qs, gs = refs[1 + count :]
+        stack_heads(qg_ref, 0, qs)
+        stack_heads(qg_ref, 1, gs)
     keys, wide = kvs[0].shape
     width = wide // 2
     lanes = qs.shape[0]
     scale = width ** (-0.5)
     trunk = keys - TILE
-    stack_heads(qg_ref, 0, qs)
-    stack_heads(qg_ref, 1, gs)
     ids = lax.broadcasted_iota(jnp.int32, (TILE, lanes), 0)
     room = jnp.broadcast_to(lim_ref[...], (TILE, lanes)) - ids
-    top = jnp.full((1, lanes), MASKED, jnp.float32)
-    total = jnp.zeros((1, lanes), jnp.float32)
-    slope = jnp.zeros((1, lanes), jnp.float32)
-    for k in range(blocks):
-        b = source(pos_ref, k, blocks)
-        e_ref[k] = dot_nt(kvs[k][:, :width], qs[...])
-        s_ref[k] = dot_nt(kvs[k][:, width:], gs[...])
+    if last:
+        top, total, slope = (before_ref[i : i + 1, :] for i in range(3))
+    else:
+        top = jnp.full((1, lanes), MASKED, jnp.float32)
+        total = jnp.zeros((1, lanes), jnp.float32)
+        slope = jnp.zeros((1, lanes), jnp.float32)
+    for i in range(count):
+        b = source(pos_ref, shifts[i], 4)
+        e_ref[i] = dot_nt(kvs[i][:, :width], qs[...])
+        s_ref[i] = dot_nt(kvs[i][:, width:], gs[...])
 
         def mask(t, best):
             at = pl.ds(pl.multiple_of(t * TILE, TILE), TILE)
-            s = jnp.where(room > b * trunk + t * TILE, e_ref[k, at, :] * scale, MASKED)
-            e_ref[k, at, :] = s
+            s = jnp.where(room > b * trunk + t * TILE, e_ref[i, at, :] * scale, MASKED)
+            e_ref[i, at, :] = s
             return jnp.maximum(best, s)
 
         best = lax.fori_loop(
@@ -80,35 +106,46 @@
         )
         tree = jnp.where(
             reach_ref[pl.ds(pl.multiple_of(b * TILE, TILE), TILE), :] > 0.5,
-            e_ref[k, pl.ds(trunk, TILE), :] * scale,
+            e_ref[i, pl.ds(trunk, TILE), :] * scale,
             MASKED,
         )
-        e_ref[k, pl.ds(trunk, TILE), :] = tree
+        e_ref[i, pl.ds(trunk, TILE), :] = tree
         best = jnp.max(jnp.maximum(best, tree), axis=0, keepdims=True)
         now = jnp.maximum(top, best)
         fade = jnp.exp(top - now)
-        tops_ref[pl.ds(k, 1), :] = now
+        tops_ref[pl.ds(i, 1), :] = now
 
         def add(t, sums):
             at = pl.ds(pl.multiple_of(t * TILE, TILE), TILE)
-            p = jnp.exp(e_ref[k, at, :] - now)
-            e_ref[k, at, :] = p
-            return (sums[0] + p, sums[1] + p * s_ref[k, at, :])
+            p = jnp.exp(e_ref[i, at, :] - now)
+            e_ref[i, at, :] = p
+            return (sums[0] + p, sums[1] + p * s_ref[i, at, :])
 
         zero = jnp.zeros((TILE, lanes), jnp.float32)
         l, d = lax.fori_loop(0, keys // TILE, add, (zero, zero), unroll=3)
         total = total * fade + jnp.sum(l, axis=0, keepdims=True)
         slope = slope * fade + jnp.sum(d, axis=0, keepdims=True)
         top = now
-    out_ref[0:1, :] = top + jnp.log(total)
-    out_ref[1:2, :] = slope / total
-
-
-def grads_kernel(pos_ref, stats_ref, tops_ref, e_ref, s_ref, qs, gs, *refs):
-    blocks, keys, lanes = e_ref.shape
-    kvs = refs[:blocks]
-    qkeep_ref, qsend_ref, keep_ref, send_ref, tkeep_ref, tsend_ref = refs[blocks : blocks + 6]
-    d_scr, p_scr, kv_scr, dq_scr, q_scr, tree_scr = refs[blocks + 6 :]
+    if last:
+        after_ref[0:1, :] = top + jnp.log(total)
+        after_ref[1:2, :] = slope / total
+    else:
+        after_ref[0:1, :] = top
+        after_ref[1:2, :] = total
+        after_ref[2:3, :] = slope
+
+
+def grads_kernel(shifts, pos_ref, stats_ref, qs, gs, *refs):
+    blocks = len(shifts[0]) + len(shifts[1])
+    kvs = refs[6 : 6 + blocks]
+    held = [
+        (k, kvs[k], refs[3 * half].at[pl.ds(i, 1)], refs[3 * half + 1].at[i], refs[3 * half + 2].at[i])
+        for half in range(2)
+        for i, k in enumerate(shifts[half])
+    ]
+    qkeep_ref, qsend_ref, keep_ref, send_ref, tkeep_ref, tsend_ref = refs[6 + blocks : 12 + blocks]
+    d_scr, p_scr, kv_scr, dq_scr, q_scr, tree_scr = refs[12 + blocks :]
+    keys, lanes = d_scr.shape
     groups = stats_ref.shape[0]
     own = qkeep_ref.shape[1]
     rows = groups * own
@@ -129,14 +166,14 @@
     delta = jnp.zeros_like(top)
     for i in range(groups):
         delta = delta + jnp.exp(parts[i] - log_total) * stats_ref[i, 1:2, :]
-    for k in range(blocks):
+    for step, (k, kv_ref, top_ref, e_ref, s_ref) in enumerate(held):
         b = source(pos_ref, k, blocks)
-        fade = jnp.exp(tops_ref[pl.ds(k, 1), :] - log_total)
+        fade = jnp.exp(top_ref[...] - log_total)
 
         def tile(t, carry):
             at = pl.ds(pl.multiple_of(t * TILE, TILE), TILE)
-            p = e_ref[k, at, :] * fade
-            d_scr[at, :] = (p * (s_ref[k, at, :] - delta)).astype(jnp.bfloat16)
+            p = e_ref[at, :] * fade
+            d_scr[at, :] = (p * (s_ref[at, :] - delta)).astype(jnp.bfloat16)
             p_scr[at, :] = p.astype(jnp.bfloat16)
             return carry
 
@@ -149,8 +186,8 @@
         tree_scr[b, :, width:] = dv[trunk:]
         keep_ref[b] = kv_scr[:, mine]
         send_ref[b] = kv_scr[:, 1 - mine].astype(jnp.bfloat16)
-        part = dot_tn(kvs[k][:, :width], d_scr[...])
-        if k == 0:
+        part = dot_tn(kv_ref[:, :width], d_scr[...])
+        if step == 0:
             dq_scr[...] = part
         else:
             dq_scr[...] += part
@@ -196,9 +233,24 @@
     lanes = rows * heads
     pos = jnp.stack([x, core, yh])
 
-    qg = spread(jnp.stack([queries[0], out_grad[0]]), "yh")
-    kv = jnp.concatenate([trunk_kv, branch_kv[0]], axis=0)
+    shape = jax.ShapeDtypeStruct
+    vmem = pl.BlockSpec(memory_space=pltpu.VMEM)
+    smem = pl.BlockSpec(memory_space=pltpu.SMEM)
+    qg, kv = pl.pallas_call(
+        pack_kernel,
+        out_shape=(
+            shape((ny, 2) + queries.shape[1:], bf16),
+            shape((trunk_kv.shape[0] + own, 2 * width), bf16),
+        ),
+        in_specs=[vmem] * 4,
+        out_specs=(pl.BlockSpec(memory_space=pl.ANY), vmem),
+        scratch_shapes=[pltpu.SemaphoreType.DMA((ny, 2))],
+        compiler_params=pltpu.CompilerParams(vmem_limit_bytes=4 << 20),
+        name="pack",
+    )(queries, out_grad, trunk_kv, branch_kv)
+    qg = swap(qg, "yh")
     kvs = [kv] + [turn(kv, "x", k) for k in range(1, nx)]
+    shifts = ((0, 1), (2, 3))
 
     mine = prefix[0].reshape(ny, nx, own)[:, x].reshape(rows)
     lim = jnp.tile(mine - yh * span, heads)[None]
@@ -208,28 +260,35 @@
     reach = jnp.tile(reach.astype(f32), (1, heads))
 
     keys = kv.shape[0]
-    vmem = pl.BlockSpec(memory_space=pltpu.VMEM)
-    smem = pl.BlockSpec(memory_space=pltpu.SMEM)
-    shape = jax.ShapeDtypeStruct
-    stats, tops, e, s, qs, gs = pl.pallas_call(
-        stats_kernel,
-        out_shape=(
-            shape((2, lanes), f32),
-            shape((nx, lanes), f32),
-            shape((nx, keys, lanes), f32),
-            shape((nx, keys, lanes), f32),
-            shape((lanes, width), bf16),
-            shape((lanes, width), bf16),
-        ),
-        in_specs=[smem] + [vmem] * (3 + nx),
-        out_specs=(vmem,) * 6,
-        compiler_params=pltpu.CompilerParams(vmem_limit_bytes=6 << 20),
-        name="stats",
-    )(pos, lim, reach, qg, *kvs)
+    head = (pos, lim, reach)
+    rest = [qg]
+    held = []
+    for half in range(2):
+        count = len(shifts[half])
+        outs = [
+            shape((3 - half, lanes), f32),
+            shape((count, lanes), f32),
+            shape((count, keys, lanes), f32),
+            shape((count, keys, lanes), f32),
+        ]
+        if half == 0:
+            outs += [shape((lanes, width), bf16)] * 2
+        stats, tops, e, s, *stacked = pl.pallas_call(
+            functools.partial(stats_kernel, shifts[half], half == 1),
+            out_shape=tuple(outs),
+            in_specs=[smem] + [vmem] * (2 + len(rest) + count),
+            out_specs=(vmem,) * len(outs),
+            compiler_params=pltpu.CompilerParams(vmem_limit_bytes=6 << 20),
+            name="stats",
+        )(*head, *rest, *[kvs[k] for k in shifts[half]])
+        held += [tops, e, s]
+        if half == 0:
+            qs, gs = stacked
+            rest = [qs, gs, stats]
     stats = spread(stats, "yh")
     pieces = trunk_kv.shape[0] // (2 * own)
     q_keep, q_send, keep, send, t_keep, t_send = pl.pallas_call(
-        grads_kernel,
+        functools.partial(grads_kernel, shifts),
         out_shape=(
             shape((ny // 2, own, heads * width), f32),
             shape((ny // 2, own, heads * width), bf16),
@@ -238,7 +297,7 @@
             shape((nx // 2, own, 2 * width), f32),
             shape((nx // 2, own, 2 * width), f32),
         ),
-        in_specs=[smem] + [vmem] * (6 + nx),
+        in_specs=[smem] + [vmem] * (9 + nx),
         out_specs=(vmem,) * 6,
         scratch_shapes=[
             pltpu.VMEM((keys, lanes), bf16),
@@ -250,7 +309,7 @@
         ],
         compiler_params=pltpu.CompilerParams(vmem_limit_bytes=10 << 20),
         name="grads",
-    )(pos, stats, tops, e, s, qs, gs, *kvs)
+    )(pos, stats, qs, gs, *held, *kvs)
     other = turn(send, "c", 1)
     trunk = (keep + other.astype(f32)).astype(bf16).reshape(nx * pieces, own, 2 * width)
     trunk = swap(trunk, ("x", "z", "yl"))

time: 106 us -> 108 us (1.019)
  other arithmetic: 6.31 us -> 3.73 us
  local copies, waits for them, and re-layouts: 2.08 us -> 4.55 us
  Pallas kernels: 15 us -> 16.2 us
    unnamed x1 -> x11, local copies, waits for them, and re-layouts: 0.51 us -> 3.83 us
    pallas_call x2 -> x4, Pallas kernels: 15 us -> 16.2 us  [the longest x2 9.17 us: per_device(): pl.pallas_call(functools.partial(stats_kernel, shifts[half], half == 1),...]
  transfers between devices with their start and end apart: 10 -> 10, of which waited for: 3 -> 3; matrix products, arithmetic and copies ran while one was open for 9% -> 6% of each run, Pallas kernels for 0% -> 4%
where the time goes in v1:
time: 108 us; the launch traced here: 107 us
  starting transfers between devices  50.7 us (47%)
  waiting for transfers between devices  19 us (18%)
  Pallas kernels  16.2 us (15%)
  blocking collectives  9.4 us (9%)
  local copies, waits for them, and re-layouts  4.55 us (4%)
  other arithmetic  3.73 us (3%)
  matrix products  2.65 us (2%)
    all_to_all x2, starting transfers between devices, swap(): return lax.all_to_all(x, axis, 0, 0)  22.6 us
    ppermute x4, starting transfers between devices, meet(): lax.ppermute(x, axis, [(i, i ^ bit) for i in range(lax.axis_size(axis))])  14.9 us
    all_to_all x2, waiting for transfers between devices, swap(): return lax.all_to_all(x, axis, 0, 0)  14.8 us
    ppermute x4, starting transfers between devices, turn(): return lax.ppermute(x, axis, [(i, (i + k) % n) for i in range(n)])  13.3 us
    all_to_all x1, blocking collectives, swap(): return lax.all_to_all(x, axis, 0, 0)  9.4 us
    pallas_call x2, Pallas kernels, per_device(): pl.pallas_call(functools.partial(stats_kernel, shifts[half], half == 1),...  9.17 us
    pallas_call x1, Pallas kernels, per_device(): pl.pallas_call(functools.partial(grads_kernel, shifts), out_shape=(shape(...  6.18 us
    ppermute x4, waiting for transfers between devices, meet(): lax.ppermute(x, axis, [(i, i ^ bit) for i in range(lax.axis_size(axis))])  4.21 us
  transfers between devices with their start and end apart: 10, of which 3 were waited for; matrix products, arithmetic and copies ran while one was open for 6% of the time, Pallas kernels for 4%

profile of v1, /device:TPU:40, one launch (start us, length us, event | category | flops | bytes accessed | tf_op | source)
XLA Modules:
  0.0 107.2 jit_solution(3478288673917575539)
XLA Ops:
  0.6 0.0 copy-start
  0.6 0.9 copy-done
  1.6 0.8 copy-done.1
  2.4 0.8 copy-done.2
  3.3 0.7 copy-done.3
  4.0 0.9 pack.1
  4.8 3.4 %collective-permute-start = (bf16[528,256]{1,0:T(8,128)(2,1)S(1)}, bf16[528,256]{1,0:T(8,128)(2,1)S(1)}, u32[]{:S(2)}, u32[]{:S(2)}) collective-permute-start(bf16[528,256]{1,0:T(8,128)(2,1)S(1)} %get-tuple-element.22.refs_1_.refs_6_), channel_id=1, source_target_pairs={{0,32},{32,64},{64,96},{96,0},{1,33},{33,65},{65,97},{97,1},{2,34}... | collective-permute-start | bytes 811016 | tf_op jit(solution)/shard_map/ppermute | solution.py:213
  8.2 4.6 %collective-permute-start.1 = (bf16[528,256]{1,0:T(8,128)(2,1)S(1)}, bf16[528,256]{1,0:T(8,128)(2,1)S(1)}, u32[]{:S(2)}, u32[]{:S(2)}) collective-permute-start(bf16[528,256]{1,0:T(8,128)(2,1)S(1)} %get-tuple-element.22.refs_1_.refs_6_), channel_id=1, source_target_pairs={{0,64},{32,96},{64,0},{96,32},{1,65},{33,97},{65,1},{97,33},{2,66}... | collective-permute-start | bytes 811016 | tf_op jit(solution)/shard_map/ppermute | solution.py:213
  12.9 3.3 %collective-permute-start.2 = (bf16[528,256]{1,0:T(8,128)(2,1)S(1)}, bf16[528,256]{1,0:T(8,128)(2,1)S(1)}, u32[]{:S(2)}, u32[]{:S(2)}) collective-permute-start(bf16[528,256]{1,0:T(8,128)(2,1)S(1)} %get-tuple-element.22.refs_1_.refs_6_), channel_id=1, source_target_pairs={{0,96},{32,0},{64,32},{96,64},{1,97},{33,1},{65,33},{97,65},{2,98}... | collective-permute-start | bytes 811016 | tf_op jit(solution)/shard_map/ppermute | solution.py:213
  16.2 7.2 %all-to-all-start = ((bf16[4,2,16,2048]{3,2,1,0:T(8,128)(2,1)}), bf16[4,2,16,2048]{3,2,1,0:T(8,128)(2,1)S(1)}, u32[]{:S(2)}, u32[]{:S(2)}) async-start(bf16[4,2,16,2048]{3,2,1,0:T(8,128)(2,1)} %get-tuple-element.21), calls=%async_computation | async-start | bytes 1048576 | tf_op jit(solution)/shard_map/all_to_all | solution.py:204
  23.4 1.3 %fusion.1 = bf16[256,256]{1,0:T(8,128)(2,1)S(1)} fusion(s32[256]{0:T(256)} %bitcast.38), kind=kOutput, calls=%fused_computation.8 | convolution fusion | flops 67567616 | bytes 132096 | tf_op jit(solution)/shard_map/dot_general | solution.py:22
  24.8 0.4 fusion.3
  25.2 0.4 fusion.5
  25.7 0.4 fusion.7
  26.2 0.1 copy.11
  26.3 0.1 copy.12
  26.4 0.2 tile.8.reach_ref
  26.6 0.5 broadcast.36
  27.1 0.0 copy-done.4
  27.1 0.7 reduce.3
  27.8 0.1 reshape_squeeze.2
  27.9 0.1 sub.21
  28.0 0.1 broadcast_in_dim_tile.3.lim_ref
  28.1 0.1 pad_add_fusion.pos_ref
  28.1 0.0 collective-permute-done.refs_2_.refs_7_
  28.1 6.6 %all-to-all-done.refs_0_ = bf16[4,2,16,2048]{3,2,1,0:T(8,128)(2,1)S(1)} async-done(((bf16[4,2,16,2048]{3,2,1,0:T(8,128)(2,1)}), bf16[4,2,16,2048]{3,2,1,0:T(8,128)(2,1)S(1)}, u32[]{:S(2)}, u32[]{:S(2)}) %all-to-all-start) | async-done | bytes 524320 | tf_op jit(solution)/shard_map/all_to_all | solution.py:204
  34.7 4.6 %stats.2 = (f32[3,1024]{1,0:T(4,128)S(1)}, f32[2,1024]{1,0:T(2,128)S(1)}, f32[2,528,1024]{2,1,0:T(8,128)S(1)}, f32[2,528,1024]{2,1,0:T(8,128)S(1)}, bf16[1024,12...) custom-call(s32[3]{0:T(128)S(1)} %pad_add_fusion.pos_ref, s32[1,1024]{1,0:T(1,128)S(1)} %broadcast_in_dim_tile.3.lim_ref, ...), custom_call_target="tpu_custom_call" | custom-call | tf_op jit(solution)/shard_map/stats/pallas_call | solution.py:276
  39.3 0.0 collective-permute-done.1.refs_3_.refs_8_
  39.3 0.0 collective-permute-done.2.refs_4_.refs_9_
  39.4 4.6 %stats.3 = (f32[2,1024]{1,0:T(2,128)S(1)}, f32[2,1024]{1,0:T(2,128)S(1)}, f32[2,528,1024]{2,1,0:T(8,128)S(1)}, f32[2,528,1024]{2,1,0:T(8,128)S(1)}) custom-call(s32[3]{0:T(128)S(1)} %pad_add_fusion.pos_ref, s32[1,1024]{1,0:T(1,128)S(1)} %broadcast_in_dim_tile.3.lim_ref, f32[64,1024]{1,0:T(8,128)S(1)} %tile.8.reach_ref, ...), custom_call_target="tpu_custom_call" | custom-call | tf_op jit(solution)/shard_map/stats/pallas_call | solution.py:276
  44.0 9.4 %all_to_all.15.stats_ref = f32[4,2,1024]{2,1,0:T(2,128)S(1)} all-to-all(f32[4,2,1024]{2,1,0:T(2,128)S(1)} %broadcast_in_dim.6), channel_id=1, replica_groups=mesh['yh'=4,'x'=4,'z'=8,'yl'=2,'c'=2] {'yh'}, dimensions={0} | all-to-all | bytes 65536 | tf_op jit(solution)/shard_map/all_to_all | solution.py:204
  53.4 6.2 %grads.1 = (f32[2,16,2048]{2,1,0:T(8,128)S(1)}, bf16[2,16,2048]{2,1,0:T(8,128)(2,1)S(1)}, f32[4,16,16,256]{3,2,1,0:T(8,128)S(1)}, bf16[4,16,16,256]{3,2,1,0:T(8,...) custom-call(s32[3]{0:T(128)S(1)} %pad_add_fusion.pos_ref, f32[4,2,1024]{2,1,0:T(2,128)S(1)} %all_to_all.15.stats_ref, ...), custom_call_target="tpu_custom_call" | custom-call | tf_op jit(solution)/shard_map/grads/pallas_call | solution.py:290
  59.5 1.9 %collective-permute-start.7 = (bf16[4,16,16,256]{3,2,1,0:T(8,128)(2,1)S(1)}, bf16[4,16,16,256]{3,2,1,0:T(8,128)(2,1)S(1)}, u32[]{:S(2)}, u32[]{:S(2)}) collective-permute-start(bf16[4,16,16,256]{3,2,1,0:T(8,128)(2,1)S(1)} %get-tuple-element.38), channel_id=1, source_target_pairs={{0,1},{1,0},{2,3},{3,2},{4,5},{5,4},{6,7},{7,6},{8,9},{9,8},{10,11... | collective-permute-start | bytes 1572872 | tf_op jit(solution)/shard_map/ppermute | solution.py:213
  61.5 2.5 %collective-permute-start.5 = (f32[2,16,256]{2,1,0:T(8,128)S(1)}, f32[2,16,256]{2,1,0:T(8,128)S(1)}, u32[]{:S(2)}, u32[]{:S(2)}) collective-permute-start(f32[2,16,256]{2,1,0:T(8,128)S(1)} %get-tuple-element.36), channel_id=1, source_target_pairs={{0,64},{32,96},{64,0},{96,32},{1,65},{33,97},{65,1},{97,33},{2,66}... | collective-permute-start | bytes 98312 | tf_op jit(solution)/shard_map/ppermute | solution.py:217
  64.0 7.4 %collective-permute-start.3 = (bf16[2,16,2048]{2,1,0:T(8,128)(2,1)S(1)}, bf16[2,16,2048]{2,1,0:T(8,128)(2,1)S(1)}, u32[]{:S(2)}, u32[]{:S(2)}) collective-permute-start(bf16[2,16,2048]{2,1,0:T(8,128)(2,1)S(1)} %get-tuple-element.34), channel_id=1, source_target_pairs={{0,256},{128,384},{256,0},{384,128},{1,257},{129,385},{257,1},{385... | collective-permute-start | bytes 393224 | tf_op jit(solution)/shard_map/ppermute | solution.py:217
  71.3 0.0 collective-permute-done.5
  71.4 2.5 %collective-permute-start.6 = (f32[16,256]{1,0:T(8,128)S(1)}, f32[16,256]{1,0:T(8,128)S(1)}, u32[]{:S(2)}, u32[]{:S(2)}) collective-permute-start(f32[16,256]{1,0:T(8,128)S(1)} %dynamic-slice_bitcast_fusion), channel_id=1, source_target_pairs={{0,32},{32,0},{64,96},{96,64},{1,33},{33,1},{65,97},{97,65},{2,34}... | collective-permute-start | bytes 49160 | tf_op jit(solution)/shard_map/ppermute | solution.py:217
  73.9 0.0 collective-permute-done.7
  73.9 1.0 add_convert_fusion
  74.9 15.3 %all-to-all-start.2 = ((bf16[64,16,256]{2,1,0:T(8,128)(2,1)}), bf16[64,16,256]{2,1,0:T(8,128)(2,1)S(1)}, u32[]{:S(2)}, u32[]{:S(2)}) async-start(bf16[64,16,256]{2,1,0:T(8,128)(2,1)} %bitcast.12), calls=%async_computation.2 | async-start | bytes 1048576 | tf_op jit(solution)/shard_map/all_to_all | solution.py:204
  90.2 0.0 collective-permute-done.3
  90.3 2.5 %collective-permute-start.4 = (bf16[16,2048]{1,0:T(8,128)(2,1)S(1)}, bf16[16,2048]{1,0:T(8,128)(2,1)S(1)}, u32[]{:S(2)}, u32[]{:S(2)}) collective-permute-start(bf16[16,2048]{1,0:T(8,128)(2,1)S(1)} %fusion.18), channel_id=1, source_target_pairs={{0,128},{128,0},{256,384},{384,256},{1,129},{129,1},{257,385},{385... | collective-permute-start | bytes 196616 | tf_op jit(solution)/shard_map/ppermute | solution.py:217
  92.8 0.0 collective-permute-done.6
  92.9 0.6 fusion.21
  93.5 4.2 %collective-permute-done.4 = bf16[16,2048]{1,0:T(8,128)(2,1)S(1)} collective-permute-done((bf16[16,2048]{1,0:T(8,128)(2,1)S(1)}, bf16[16,2048]{1,0:T(8,128)(2,1)S(1)}, u32[]{:S(2)}, u32[]{:S(2)}) %collective-permute-start.4) | collective-permute-done | bytes 65568 | tf_op jit(solution)/shard_map/ppermute | solution.py:217
  97.7 0.6 fusion.19
  98.3 8.2 %all-to-all-done.2 = bf16[64,16,256]{2,1,0:T(8,128)(2,1)S(1)} async-done(((bf16[64,16,256]{2,1,0:T(8,128)(2,1)}), bf16[64,16,256]{2,1,0:T(8,128)(2,1)S(1)}, u32[]{:S(2)}, u32[]{:S(2)}) %all-to-all-start.2) | async-done | bytes 524320 | tf_op jit(solution)/shard_map/all_to_all | solution.py:204
  106.5 0.7 convert_reduce_fusion
  (16 shorter events, 0.2 us)
Async XLA Ops:
  0.6 1.0 copy-start
  1.6 0.8 copy-start.1
  2.4 0.8 copy-start.2
  3.3 0.7 copy-start.3
  4.0 23.2 %copy-start.4 = (s32[1,256]{1,0:T(1,128)S(1)}, s32[1,256]{1,0:T(1,128)}, u32[]{:S(2)}) copy-start(s32[1,256]{1,0:T(1,128)} %param.11) | copy-start | bytes 3076
  4.8 23.3 %collective-permute-start = (bf16[528,256]{1,0:T(8,128)(2,1)S(1)}, bf16[528,256]{1,0:T(8,128)(2,1)S(1)}, u32[]{:S(2)}, u32[]{:S(2)}) collective-permute-start(bf16[528,256]{1,0:T(8,128)(2,1)S(1)} %get-tuple-element.22.refs_1_.refs_6_), channel_id=1, source_target_pairs={{0,32},{32,64},{64,96},{96,0},{1,33},{33,65},{65,97},{97,1},{2,34}... | collective-permute-start | bytes 811016 | tf_op jit(solution)/shard_map/ppermute | solution.py:213
  8.2 31.1 %collective-permute-start.1 = (bf16[528,256]{1,0:T(8,128)(2,1)S(1)}, bf16[528,256]{1,0:T(8,128)(2,1)S(1)}, u32[]{:S(2)}, u32[]{:S(2)}) collective-permute-start(bf16[528,256]{1,0:T(8,128)(2,1)S(1)} %get-tuple-element.22.refs_1_.refs_6_), channel_id=1, source_target_pairs={{0,64},{32,96},{64,0},{96,32},{1,65},{33,97},{65,1},{97,33},{2,66}... | collective-permute-start | bytes 811016 | tf_op jit(solution)/shard_map/ppermute | solution.py:213
  12.9 26.5 %collective-permute-start.2 = (bf16[528,256]{1,0:T(8,128)(2,1)S(1)}, bf16[528,256]{1,0:T(8,128)(2,1)S(1)}, u32[]{:S(2)}, u32[]{:S(2)}) collective-permute-start(bf16[528,256]{1,0:T(8,128)(2,1)S(1)} %get-tuple-element.22.refs_1_.refs_6_), channel_id=1, source_target_pairs={{0,96},{32,0},{64,32},{96,64},{1,97},{33,1},{65,33},{97,65},{2,98}... | collective-permute-start | bytes 811016 | tf_op jit(solution)/shard_map/ppermute | solution.py:213
  16.2 18.5 %all-to-all-start = ((bf16[4,2,16,2048]{3,2,1,0:T(8,128)(2,1)}), bf16[4,2,16,2048]{3,2,1,0:T(8,128)(2,1)S(1)}, u32[]{:S(2)}, u32[]{:S(2)}) async-start(bf16[4,2,16,2048]{3,2,1,0:T(8,128)(2,1)} %get-tuple-element.21), calls=%async_computation | async-start | bytes 1048576 | tf_op jit(solution)/shard_map/all_to_all | solution.py:204
  59.5 14.4 %collective-permute-start.7 = (bf16[4,16,16,256]{3,2,1,0:T(8,128)(2,1)S(1)}, bf16[4,16,16,256]{3,2,1,0:T(8,128)(2,1)S(1)}, u32[]{:S(2)}, u32[]{:S(2)}) collective-permute-start(bf16[4,16,16,256]{3,2,1,0:T(8,128)(2,1)S(1)} %get-tuple-element.38), channel_id=1, source_target_pairs={{0,1},{1,0},{2,3},{3,2},{4,5},{5,4},{6,7},{7,6},{8,9},{9,8},{10,11... | collective-permute-start | bytes 1572872 | tf_op jit(solution)/shard_map/ppermute | solution.py:213
  61.5 9.9 %collective-permute-start.5 = (f32[2,16,256]{2,1,0:T(8,128)S(1)}, f32[2,16,256]{2,1,0:T(8,128)S(1)}, u32[]{:S(2)}, u32[]{:S(2)}) collective-permute-start(f32[2,16,256]{2,1,0:T(8,128)S(1)} %get-tuple-element.36), channel_id=1, source_target_pairs={{0,64},{32,96},{64,0},{96,32},{1,65},{33,97},{65,1},{97,33},{2,66}... | collective-permute-start | bytes 98312 | tf_op jit(solution)/shard_map/ppermute | solution.py:217
  64.0 26.3 %collective-permute-start.3 = (bf16[2,16,2048]{2,1,0:T(8,128)(2,1)S(1)}, bf16[2,16,2048]{2,1,0:T(8,128)(2,1)S(1)}, u32[]{:S(2)}, u32[]{:S(2)}) collective-permute-start(bf16[2,16,2048]{2,1,0:T(8,128)(2,1)S(1)} %get-tuple-element.34), channel_id=1, source_target_pairs={{0,256},{128,384},{256,0},{384,128},{1,257},{129,385},{257,1},{385... | collective-permute-start | bytes 393224 | tf_op jit(solution)/shard_map/ppermute | solution.py:217
  71.4 21.5 %collective-permute-start.6 = (f32[16,256]{1,0:T(8,128)S(1)}, f32[16,256]{1,0:T(8,128)S(1)}, u32[]{:S(2)}, u32[]{:S(2)}) collective-permute-start(f32[16,256]{1,0:T(8,128)S(1)} %dynamic-slice_bitcast_fusion), channel_id=1, source_target_pairs={{0,32},{32,0},{64,96},{96,64},{1,33},{33,1},{65,97},{97,65},{2,34}... | collective-permute-start | bytes 49160 | tf_op jit(solution)/shard_map/ppermute | solution.py:217
  74.9 31.7 %all-to-all-start.2 = ((bf16[64,16,256]{2,1,0:T(8,128)(2,1)}), bf16[64,16,256]{2,1,0:T(8,128)(2,1)S(1)}, u32[]{:S(2)}, u32[]{:S(2)}) async-start(bf16[64,16,256]{2,1,0:T(8,128)(2,1)} %bitcast.12), calls=%async_computation.2 | async-start | bytes 1048576 | tf_op jit(solution)/shard_map/all_to_all | solution.py:204
  90.3 7.4 %collective-permute-start.4 = (bf16[16,2048]{1,0:T(8,128)(2,1)S(1)}, bf16[16,2048]{1,0:T(8,128)(2,1)S(1)}, u32[]{:S(2)}, u32[]{:S(2)}) collective-permute-start(bf16[16,2048]{1,0:T(8,128)(2,1)S(1)} %fusion.18), channel_id=1, source_target_pairs={{0,128},{128,0},{256,384},{384,256},{1,129},{129,1},{257,385},{385... | collective-permute-start | bytes 196616 | tf_op jit(solution)/shard_map/ppermute | solution.py:217

commit v2 on v1

--- a/solution.py
+++ b/solution.py
@@ -50,19 +50,28 @@
     return lax.rem(pos_ref[0] + blocks - k, blocks)
 
 
-def pack_kernel(q_ref, g_ref, trunk_ref, branch_ref, qg_ref, kv_ref, sems):
-    copies = [
-        pltpu.make_async_copy(part.at[0], qg_ref.at[y, i], sems.at[y, i])
-        for y in range(qg_ref.shape[0])
-        for i, part in enumerate((q_ref, g_ref))
+def pack_kernel(q_ref, g_ref, trunk_ref, branch_ref, qg_ref, kv_ref, held, load_sems, sems):
+    trunk = trunk_ref.shape[0]
+    loads = [
+        pltpu.make_async_copy(q_ref.at[0], held.at[0], load_sems.at[0]),
+        pltpu.make_async_copy(g_ref.at[0], held.at[1], load_sems.at[1]),
+        pltpu.make_async_copy(trunk_ref, kv_ref.at[pl.ds(0, trunk)], load_sems.at[2]),
+        pltpu.make_async_copy(
+            branch_ref.at[0], kv_ref.at[pl.ds(trunk, branch_ref.shape[1])], load_sems.at[3]
+        ),
     ]
-    for copy in copies:
-        copy.start()
-    trunk = trunk_ref.shape[0]
-    kv_ref[:trunk, :] = trunk_ref[...]
-    kv_ref[trunk:, :] = branch_ref[0]
-    for copy in copies:
-        copy.wait()
+    for load in loads:
+        load.start()
+    stores = []
+    for i in range(2):
+        loads[i].wait()
+        for y in range(qg_ref.shape[0]):
+            stores.append(pltpu.make_async_copy(held.at[i], qg_ref.at[y, i], sems.at[y, i]))
+            stores[-1].start()
+    for load in loads[2:]:
+        load.wait()
+    for store in stores:
+        store.wait()
 
 
 def stats_kernel(shifts, last, pos_ref, lim_ref, reach_ref, *refs):
@@ -143,8 +152,8 @@
         for half in range(2)
         for i, k in enumerate(shifts[half])
     ]
-    qkeep_ref, qsend_ref, keep_ref, send_ref, tkeep_ref, tsend_ref = refs[6 + blocks : 12 + blocks]
-    d_scr, p_scr, kv_scr, dq_scr, q_scr, tree_scr = refs[12 + blocks :]
+    qkeep_ref, qsend_ref, part_ref = refs[6 + blocks : 9 + blocks]
+    d_scr, p_scr, part_scr, dq_scr, q_scr, sems = refs[9 + blocks :]
     keys, lanes = d_scr.shape
     groups = stats_ref.shape[0]
     own = qkeep_ref.shape[1]
@@ -154,7 +163,6 @@
     trunk = keys - TILE
     mine = pos_ref[1]
     q_half = lax.div(pos_ref[2], 2)
-    tree_half = lax.div(pos_ref[0], 2)
     parts = [stats_ref[i, 0:1, :] for i in range(groups)]
     top = parts[0]
     for part in parts[1:]:
@@ -166,6 +174,7 @@
     delta = jnp.zeros_like(top)
     for i in range(groups):
         delta = delta + jnp.exp(parts[i] - log_total) * stats_ref[i, 1:2, :]
+    copies = []
     for step, (k, kv_ref, top_ref, e_ref, s_ref) in enumerate(held):
         b = source(pos_ref, k, blocks)
         fade = jnp.exp(top_ref[...] - log_total)
@@ -180,12 +189,19 @@
         lax.fori_loop(0, keys // TILE, tile, 0, unroll=3)
         dk = scale * jnp.dot(d_scr[...], qs[...], preferred_element_type=jnp.float32)
         dv = jnp.dot(p_scr[...], gs[...], preferred_element_type=jnp.float32)
-        kv_scr[:, :, :, :width] = dk[:trunk].reshape(trunk // (2 * TILE), 2, TILE, width)
-        kv_scr[:, :, :, width:] = dv[:trunk].reshape(trunk // (2 * TILE), 2, TILE, width)
-        tree_scr[b, :, :width] = dk[trunk:]
-        tree_scr[b, :, width:] = dv[trunk:]
-        keep_ref[b] = kv_scr[:, mine]
-        send_ref[b] = kv_scr[:, 1 - mine].astype(jnp.bfloat16)
+        for half, grad in enumerate((dk, dv)):
+            at = pl.ds(half * width, width)
+            grad = grad.astype(jnp.bfloat16)
+            for piece in range(trunk // TILE):
+                part_scr[step, piece % 2, pl.ds(piece // 2 * TILE, TILE), at] = grad[
+                    piece * TILE : (piece + 1) * TILE
+                ]
+            for core in range(2):
+                part_scr[step, core, pl.ds(trunk // 2, TILE), at] = jnp.where(
+                    core == mine, grad[trunk:], jnp.zeros_like(grad[trunk:])
+                )
+        copies.append(pltpu.make_async_copy(part_scr.at[step], part_ref.at[b], sems.at[step]))
+        copies[-1].start()
         part = dot_tn(kv_ref[:, :width], d_scr[...])
         if step == 0:
             dq_scr[...] = part
@@ -196,8 +212,8 @@
         q_scr[:, :, pl.ds(h * width, width)] = piece.reshape(groups, own, width)
     qkeep_ref[...] = q_scr[pl.ds(2 * q_half, 2)]
     qsend_ref[...] = q_scr[pl.ds(2 - 2 * q_half, 2)].astype(jnp.bfloat16)
-    tkeep_ref[...] = tree_scr[pl.ds(2 * tree_half, 2)]
-    tsend_ref[...] = tree_scr[pl.ds(2 - 2 * tree_half, 2)]
+    for copy in copies:
+        copy.wait()
 
 
 def swap(x, axis):
@@ -236,16 +252,20 @@
     shape = jax.ShapeDtypeStruct
     vmem = pl.BlockSpec(memory_space=pltpu.VMEM)
     smem = pl.BlockSpec(memory_space=pltpu.SMEM)
+    anywhere = pl.BlockSpec(memory_space=pl.ANY)
     qg, kv = pl.pallas_call(
         pack_kernel,
         out_shape=(
             shape((ny, 2) + queries.shape[1:], bf16),
             shape((trunk_kv.shape[0] + own, 2 * width), bf16),
         ),
-        in_specs=[vmem] * 4,
-        out_specs=(pl.BlockSpec(memory_space=pl.ANY), vmem),
-        scratch_shapes=[pltpu.SemaphoreType.DMA((ny, 2))],
-        compiler_params=pltpu.CompilerParams(vmem_limit_bytes=4 << 20),
+        in_specs=[anywhere] * 4,
+        out_specs=(anywhere, vmem),
+        scratch_shapes=[
+            pltpu.VMEM((2,) + queries.shape[1:], bf16),
+            pltpu.SemaphoreType.DMA((4,)),
+            pltpu.SemaphoreType.DMA((ny, 2)),
+        ],
         name="pack",
     )(queries, out_grad, trunk_kv, branch_kv)
     qg = swap(qg, "yh")
@@ -286,40 +306,36 @@
             qs, gs = stacked
             rest = [qs, gs, stats]
     stats = spread(stats, "yh")
-    pieces = trunk_kv.shape[0] // (2 * own)
-    q_keep, q_send, keep, send, t_keep, t_send = pl.pallas_call(
+    half_keys = trunk_kv.shape[0] // 2
+    q_keep, q_send, part = pl.pallas_call(
         functools.partial(grads_kernel, shifts),
         out_shape=(
             shape((ny // 2, own, heads * width), f32),
             shape((ny // 2, own, heads * width), bf16),
-            shape((nx, pieces, own, 2 * width), f32),
-            shape((nx, pieces, own, 2 * width), bf16),
-            shape((nx // 2, own, 2 * width), f32),
-            shape((nx // 2, own, 2 * width), f32),
+            shape((nx, 2, half_keys + own, 2 * width), bf16),
         ),
         in_specs=[smem] + [vmem] * (9 + nx),
-        out_specs=(vmem,) * 6,
+        out_specs=(vmem, vmem, anywhere),
         scratch_shapes=[
             pltpu.VMEM((keys, lanes), bf16),
             pltpu.VMEM((keys, lanes), bf16),
-            pltpu.VMEM((pieces, 2, own, 2 * width), f32),
+            pltpu.VMEM((nx, 2, half_keys + own, 2 * width), bf16),
             pltpu.VMEM((width, lanes), f32),
             pltpu.VMEM((ny, own, heads * width), f32),
-            pltpu.VMEM((nx, own, 2 * width), f32),
+            pltpu.SemaphoreType.DMA((nx,)),
         ],
         compiler_params=pltpu.CompilerParams(vmem_limit_bytes=10 << 20),
         name="grads",
     )(pos, stats, qs, gs, *held, *kvs)
-    other = turn(send, "c", 1)
-    trunk = (keep + other.astype(f32)).astype(bf16).reshape(nx * pieces, own, 2 * width)
-    trunk = swap(trunk, ("x", "z", "yl"))
+    part = swap(part.reshape(nx * 2, half_keys + own, 2 * width), ("x", "c"))
+    part = jnp.sum(part.astype(f32), axis=0)
+    branch = part[half_keys:]
+    trunk = part[:half_keys].astype(bf16).reshape(half_keys // own, own, 2 * width)
+    trunk = swap(trunk, ("z", "yl"))
     low = lax.rem(yh, 2)
     part = q_keep + meet(q_send, "yh", 2).astype(f32)
     query_grad = pick(part, low) + meet(pick(part, 1 - low).astype(bf16), "yh", 1).astype(f32)
     query_grad = query_grad.astype(bf16)
-    low = lax.rem(x, 2)
-    part = t_keep + meet(t_send, "x", 2)
-    branch = pick(part, low) + meet(pick(part, 1 - low), "x", 1)
     trunk = jnp.sum(trunk.astype(f32), axis=0)
     return (query_grad[None], branch[None], trunk)
 

time: 108 us -> 106 us (0.981)
  the two profiles are of different devices: /device:TPU:40 before, /device:TPU:2 now
where the time goes in v2:
time: 106 us; the launch traced here: 105 us
  starting transfers between devices  40.6 us (38%)
  waiting for transfers between devices  26.6 us (25%)
  Pallas kernels  17.9 us (17%)
  blocking collectives  11.7 us (11%)
  matrix products  2.65 us (2%)
  local copies, waits for them, and re-layouts  2.5 us (2%)
  other arithmetic  2.22 us (2%)
    all_to_all x3, starting transfers between devices, swap(): return lax.all_to_all(x, axis, 0, 0)  19.2 us
    all_to_all x3, waiting for transfers between devices, swap(): return lax.all_to_all(x, axis, 0, 0)  17.5 us
    ppermute x3, starting transfers between devices, turn(): return lax.ppermute(x, axis, [(i, (i + k) % n) for i in range(n)])  13.8 us
    all_to_all x1, blocking collectives, swap(): return lax.all_to_all(x, axis, 0, 0)  11.7 us
    pallas_call x2, Pallas kernels, per_device(): pl.pallas_call(functools.partial(stats_kernel, shifts[half], half == 1),...  9.17 us
    ppermute x2, waiting for transfers between devices, meet(): lax.ppermute(x, axis, [(i, i ^ bit) for i in range(lax.axis_size(axis))])  9.05 us
    ppermute x2, starting transfers between devices, meet(): lax.ppermute(x, axis, [(i, i ^ bit) for i in range(lax.axis_size(axis))])  7.52 us
    pallas_call x1, Pallas kernels, per_device(): pl.pallas_call(functools.partial(grads_kernel, shifts), out_shape=(shape(...  6.27 us
  transfers between devices with their start and end apart: 8, of which 3 were waited for; matrix products, arithmetic and copies ran while one was open for 6% of the time, Pallas kernels for 4%

profile of v2, /device:TPU:2, one launch (start us, length us, event | category | flops | bytes accessed | tf_op | source)
XLA Modules:
  0.0 105.0 jit_solution(1089842847568676196)
XLA Ops:
  0.6 0.0 copy-start.1
  0.6 2.5 %pack.1 = (bf16[4,2,16,2048]{3,2,1,0:T(8,128)(2,1)}, bf16[528,256]{1,0:T(8,128)(2,1)}) custom-call(bf16[1,16,2048]{2,1,0:T(8,128)(2,1)} %q_ref.1, bf16[1,16,2048]{2,1,0:T(8,128)(2,1)} %g_ref.1, bf16[512,256]{1,0:T(8,128)(2,1)} %trunk_ref.1, bf16[1,16,256]{2,1,0:T(8,128)(2,1)} %branch_ref.1), custom_call_target="tpu_custom_call" | custom-call | tf_op jit(solution)/shard_map/pack/pallas_call | solution.py:256
  3.1 0.0 copy-start
  3.1 3.5 %collective-permute-start = (bf16[528,256]{1,0:T(8,128)(2,1)}, bf16[528,256]{1,0:T(8,128)(2,1)S(1)}, u32[]{:S(2)}, u32[]{:S(2)}) collective-permute-start(bf16[528,256]{1,0:T(8,128)(2,1)} %get-tuple-element.19.refs_1_.refs_6_), channel_id=1, source_target_pairs={{0,32},{32,64},{64,96},{96,0},{1,33},{33,65},{65,97},{97,1},{2,34}... | collective-permute-start | bytes 811016 | tf_op jit(solution)/shard_map/ppermute | solution.py:229
  6.7 8.4 %collective-permute-start.1 = (bf16[528,256]{1,0:T(8,128)(2,1)}, bf16[528,256]{1,0:T(8,128)(2,1)S(1)}, u32[]{:S(2)}, u32[]{:S(2)}) collective-permute-start(bf16[528,256]{1,0:T(8,128)(2,1)} %get-tuple-element.19.refs_1_.refs_6_), channel_id=1, source_target_pairs={{0,64},{32,96},{64,0},{96,32},{1,65},{33,97},{65,1},{97,33},{2,66}... | collective-permute-start | bytes 811016 | tf_op jit(solution)/shard_map/ppermute | solution.py:229
  15.1 1.9 %collective-permute-start.2 = (bf16[528,256]{1,0:T(8,128)(2,1)}, bf16[528,256]{1,0:T(8,128)(2,1)S(1)}, u32[]{:S(2)}, u32[]{:S(2)}) collective-permute-start(bf16[528,256]{1,0:T(8,128)(2,1)} %get-tuple-element.19.refs_1_.refs_6_), channel_id=1, source_target_pairs={{0,96},{32,0},{64,32},{96,64},{1,97},{33,1},{65,33},{97,65},{2,98}... | collective-permute-start | bytes 811016 | tf_op jit(solution)/shard_map/ppermute | solution.py:229
  17.0 3.9 %all-to-all-start = ((bf16[4,2,16,2048]{3,2,1,0:T(8,128)(2,1)}), bf16[4,2,16,2048]{3,2,1,0:T(8,128)(2,1)S(1)}, u32[]{:S(2)}, u32[]{:S(2)}) async-start(bf16[4,2,16,2048]{3,2,1,0:T(8,128)(2,1)} %get-tuple-element.18), calls=%async_computation | async-start | bytes 1048576 | tf_op jit(solution)/shard_map/all_to_all | solution.py:220
  20.9 1.3 %fusion.1 = bf16[256,256]{1,0:T(8,128)(2,1)S(1)} fusion(s32[256]{0:T(256)} %bitcast.33), kind=kOutput, calls=%fused_computation.9 | convolution fusion | flops 67567616 | bytes 132096 | tf_op jit(solution)/shard_map/dot_general | solution.py:22
  22.2 0.4 fusion.3
  22.7 0.4 fusion.5
  23.1 0.4 fusion.7
  23.6 0.1 copy.11
  23.8 0.1 copy.12
  23.9 0.2 tile.8.reach_ref
  24.1 0.5 broadcast.35
  24.6 0.0 copy-done.1
  24.6 0.7 reduce.3
  25.2 0.1 reshape_squeeze.2
  25.3 0.1 sub.18
  25.4 0.1 broadcast_in_dim_tile.3.lim_ref
  25.5 0.1 pad_add_fusion.pos_ref
  25.6 0.0 collective-permute-done.refs_2_.refs_7_
  25.6 9.7 %all-to-all-done.refs_0_ = bf16[4,2,16,2048]{3,2,1,0:T(8,128)(2,1)S(1)} async-done(((bf16[4,2,16,2048]{3,2,1,0:T(8,128)(2,1)}), bf16[4,2,16,2048]{3,2,1,0:T(8,128)(2,1)S(1)}, u32[]{:S(2)}, u32[]{:S(2)}) %all-to-all-start) | async-done | bytes 524320 | tf_op jit(solution)/shard_map/all_to_all | solution.py:220
  35.3 0.0 copy-done
  35.3 4.6 %stats.2 = (f32[3,1024]{1,0:T(4,128)S(1)}, f32[2,1024]{1,0:T(2,128)S(1)}, f32[2,528,1024]{2,1,0:T(8,128)S(1)}, f32[2,528,1024]{2,1,0:T(8,128)S(1)}, bf16[1024,12...) custom-call(s32[3]{0:T(128)S(1)} %pad_add_fusion.pos_ref, s32[1,1024]{1,0:T(1,128)S(1)} %broadcast_in_dim_tile.3.lim_ref, ...), custom_call_target="tpu_custom_call" | custom-call | tf_op jit(solution)/shard_map/stats/pallas_call | solution.py:296
  39.9 0.0 collective-permute-done.1.refs_3_.refs_8_
  39.9 0.0 collective-permute-done.2.refs_4_.refs_9_
  39.9 4.6 %stats.3 = (f32[2,1024]{1,0:T(2,128)S(1)}, f32[2,1024]{1,0:T(2,128)S(1)}, f32[2,528,1024]{2,1,0:T(8,128)S(1)}, f32[2,528,1024]{2,1,0:T(8,128)S(1)}) custom-call(s32[3]{0:T(128)S(1)} %pad_add_fusion.pos_ref, s32[1,1024]{1,0:T(1,128)S(1)} %broadcast_in_dim_tile.3.lim_ref, f32[64,1024]{1,0:T(8,128)S(1)} %tile.8.reach_ref, ...), custom_call_target="tpu_custom_call" | custom-call | tf_op jit(solution)/shard_map/stats/pallas_call | solution.py:296
  44.5 11.7 %all_to_all.20.stats_ref = f32[4,2,1024]{2,1,0:T(2,128)S(1)} all-to-all(f32[4,2,1024]{2,1,0:T(2,128)S(1)} %broadcast_in_dim.6), channel_id=1, replica_groups=mesh['yh'=4,'x'=4,'z'=8,'yl'=2,'c'=2] {'yh'}, dimensions={0} | all-to-all | bytes 65536 | tf_op jit(solution)/shard_map/all_to_all | solution.py:220
  56.3 6.3 %grads.1 = (f32[2,16,2048]{2,1,0:T(8,128)S(1)}, bf16[2,16,2048]{2,1,0:T(8,128)(2,1)S(1)}, bf16[4,2,272,256]{3,2,1,0:T(8,128)(2,1)}) custom-call(s32[3]{0:T(128)S(1)} %pad_add_fusion.pos_ref, f32[4,2,1024]{2,1,0:T(2,128)S(1)} %all_to_all.20.stats_ref, bf16[1024,128]{1,0:T(8,128)(2,1)S(1)} %get-tuple-element.20.refs_0_.qs, ...), custom_call_target="tpu_custom_call" | custom-call | tf_op jit(solution)/shard_map/grads/pallas_call | solution.py:310
  62.5 4.9 %all-to-all-start.2 = ((bf16[8,272,256]{2,1,0:T(8,128)(2,1)}), bf16[8,272,256]{2,1,0:T(8,128)(2,1)S(1)}, u32[]{:S(2)}, u32[]{:S(2)}) async-start(bf16[8,272,256]{2,1,0:T(8,128)(2,1)} %bitcast.9), calls=%async_computation.2 | async-start | bytes 2228224 | tf_op jit(solution)/shard_map/all_to_all | solution.py:220
  67.4 2.4 %collective-permute-start.3 = (bf16[2,16,2048]{2,1,0:T(8,128)(2,1)S(1)}, bf16[2,16,2048]{2,1,0:T(8,128)(2,1)S(1)}, u32[]{:S(2)}, u32[]{:S(2)}) collective-permute-start(bf16[2,16,2048]{2,1,0:T(8,128)(2,1)S(1)} %get-tuple-element.31), channel_id=1, source_target_pairs={{0,256},{128,384},{256,0},{384,128},{1,257},{129,385},{257,1},{385... | collective-permute-start | bytes 393224 | tf_op jit(solution)/shard_map/ppermute | solution.py:233
  69.8 9.0 %collective-permute-done.3 = bf16[2,16,2048]{2,1,0:T(8,128)(2,1)S(1)} collective-permute-done((bf16[2,16,2048]{2,1,0:T(8,128)(2,1)S(1)}, bf16[2,16,2048]{2,1,0:T(8,128)(2,1)S(1)}, u32[]{:S(2)}, u32[]{:S(2)}) %collective-permute-start.3) | collective-permute-done | bytes 131104 | tf_op jit(solution)/shard_map/ppermute | solution.py:233
  78.9 5.2 %collective-permute-start.4 = (bf16[16,2048]{1,0:T(8,128)(2,1)S(1)}, bf16[16,2048]{1,0:T(8,128)(2,1)S(1)}, u32[]{:S(2)}, u32[]{:S(2)}) collective-permute-start(bf16[16,2048]{1,0:T(8,128)(2,1)S(1)} %fusion.18), channel_id=1, source_target_pairs={{0,128},{128,0},{256,384},{384,256},{1,129},{129,1},{257,385},{385... | collective-permute-start | bytes 196616 | tf_op jit(solution)/shard_map/ppermute | solution.py:233
  84.1 0.0 all-to-all-done.2
  84.1 0.1 convert_reduce_fusion
  84.2 0.7 slice.13
  84.9 10.4 %all-to-all-start.3 = ((bf16[16,16,256]{2,1,0:T(8,128)(2,1)}), bf16[16,16,256]{2,1,0:T(8,128)(2,1)S(1)}, u32[]{:S(2)}, u32[]{:S(2)}) async-start(bf16[16,16,256]{2,1,0:T(8,128)(2,1)} %bitcast.11), calls=%async_computation.3 | async-start | bytes 262144 | tf_op jit(solution)/shard_map/all_to_all | solution.py:220
  95.3 0.0 collective-permute-done.4
  95.4 0.6 fusion.19
  96.0 0.6 slice_bitcast_fusion
  96.6 7.8 %all-to-all-done.3 = bf16[16,16,256]{2,1,0:T(8,128)(2,1)S(1)} async-done(((bf16[16,16,256]{2,1,0:T(8,128)(2,1)}), bf16[16,16,256]{2,1,0:T(8,128)(2,1)S(1)}, u32[]{:S(2)}, u32[]{:S(2)}) %all-to-all-start.3) | async-done | bytes 131104 | tf_op jit(solution)/shard_map/all_to_all | solution.py:220
  104.4 0.6 convert_reduce_fusion.1
  (10 shorter events, 0.2 us)
Async XLA Ops:
  0.6 23.9 %copy-start.1 = (s32[1,256]{1,0:T(1,128)S(1)}, s32[1,256]{1,0:T(1,128)}, u32[]{:S(2)}) copy-start(s32[1,256]{1,0:T(1,128)} %param.11) | copy-start | bytes 3076
  3.1 32.2 %copy-start = (bf16[528,256]{1,0:T(8,128)(2,1)S(1)}, bf16[528,256]{1,0:T(8,128)(2,1)}, u32[]{:S(2)}) copy-start(bf16[528,256]{1,0:T(8,128)(2,1)} %get-tuple-element.19.refs_1_.refs_6_) | copy-start | bytes 811012
  3.1 22.4 %collective-permute-start = (bf16[528,256]{1,0:T(8,128)(2,1)}, bf16[528,256]{1,0:T(8,128)(2,1)S(1)}, u32[]{:S(2)}, u32[]{:S(2)}) collective-permute-start(bf16[528,256]{1,0:T(8,128)(2,1)} %get-tuple-element.19.refs_1_.refs_6_), channel_id=1, source_target_pairs={{0,32},{32,64},{64,96},{96,0},{1,33},{33,65},{65,97},{97,1},{2,34}... | collective-permute-start | bytes 811016 | tf_op jit(solution)/shard_map/ppermute | solution.py:229
  6.7 33.2 %collective-permute-start.1 = (bf16[528,256]{1,0:T(8,128)(2,1)}, bf16[528,256]{1,0:T(8,128)(2,1)S(1)}, u32[]{:S(2)}, u32[]{:S(2)}) collective-permute-start(bf16[528,256]{1,0:T(8,128)(2,1)} %get-tuple-element.19.refs_1_.refs_6_), channel_id=1, source_target_pairs={{0,64},{32,96},{64,0},{96,32},{1,65},{33,97},{65,1},{97,33},{2,66}... | collective-permute-start | bytes 811016 | tf_op jit(solution)/shard_map/ppermute | solution.py:229
  15.1 24.9 %collective-permute-start.2 = (bf16[528,256]{1,0:T(8,128)(2,1)}, bf16[528,256]{1,0:T(8,128)(2,1)S(1)}, u32[]{:S(2)}, u32[]{:S(2)}) collective-permute-start(bf16[528,256]{1,0:T(8,128)(2,1)} %get-tuple-element.19.refs_1_.refs_6_), channel_id=1, source_target_pairs={{0,96},{32,0},{64,32},{96,64},{1,97},{33,1},{65,33},{97,65},{2,98}... | collective-permute-start | bytes 811016 | tf_op jit(solution)/shard_map/ppermute | solution.py:229
  17.0 18.3 %all-to-all-start = ((bf16[4,2,16,2048]{3,2,1,0:T(8,128)(2,1)}), bf16[4,2,16,2048]{3,2,1,0:T(8,128)(2,1)S(1)}, u32[]{:S(2)}, u32[]{:S(2)}) async-start(bf16[4,2,16,2048]{3,2,1,0:T(8,128)(2,1)} %get-tuple-element.18), calls=%async_computation | async-start | bytes 1048576 | tf_op jit(solution)/shard_map/all_to_all | solution.py:220
  62.5 21.6 %all-to-all-start.2 = ((bf16[8,272,256]{2,1,0:T(8,128)(2,1)}), bf16[8,272,256]{2,1,0:T(8,128)(2,1)S(1)}, u32[]{:S(2)}, u32[]{:S(2)}) async-start(bf16[8,272,256]{2,1,0:T(8,128)(2,1)} %bitcast.9), calls=%async_computation.2 | async-start | bytes 2228224 | tf_op jit(solution)/shard_map/all_to_all | solution.py:220
  67.4 11.4 %collective-permute-start.3 = (bf16[2,16,2048]{2,1,0:T(8,128)(2,1)S(1)}, bf16[2,16,2048]{2,1,0:T(8,128)(2,1)S(1)}, u32[]{:S(2)}, u32[]{:S(2)}) collective-permute-start(bf16[2,16,2048]{2,1,0:T(8,128)(2,1)S(1)} %get-tuple-element.31), channel_id=1, source_target_pairs={{0,256},{128,384},{256,0},{384,128},{1,257},{129,385},{257,1},{385... | collective-permute-start | bytes 393224 | tf_op jit(solution)/shard_map/ppermute | solution.py:233
  78.9 16.4 %collective-permute-start.4 = (bf16[16,2048]{1,0:T(8,128)(2,1)S(1)}, bf16[16,2048]{1,0:T(8,128)(2,1)S(1)}, u32[]{:S(2)}, u32[]{:S(2)}) collective-permute-start(bf16[16,2048]{1,0:T(8,128)(2,1)S(1)} %fusion.18), channel_id=1, source_target_pairs={{0,128},{128,0},{256,384},{384,256},{1,129},{129,1},{257,385},{385... | collective-permute-start | bytes 196616 | tf_op jit(solution)/shard_map/ppermute | solution.py:233
  84.9 19.5 %all-to-all-start.3 = ((bf16[16,16,256]{2,1,0:T(8,128)(2,1)}), bf16[16,16,256]{2,1,0:T(8,128)(2,1)S(1)}, u32[]{:S(2)}, u32[]{:S(2)}) async-start(bf16[16,16,256]{2,1,0:T(8,128)(2,1)} %bitcast.11), calls=%async_computation.3 | async-start | bytes 262144 | tf_op jit(solution)/shard_map/all_to_all | solution.py:220

commit v3 on v2

v3 whole, which is shorter than its diff:
```python
import functools
import math

import jax
import jax.numpy as jnp
from jax import lax
from jax.experimental import pallas as pl
from jax.experimental.pallas import tpu as pltpu
from jax.sharding import Mesh, PartitionSpec as P


MASKED = -1e30
TILE = 16
STRIP = 8
SET = ("z", "yl", "c")


def dot_nt(left, right):
    return lax.dot_general(
        left, right, (((1,), (1,)), ((), ())), preferred_element_type=jnp.float32
    )


def dot_tn(left, right):
    return lax.dot_general(
        left, right, (((0,), (0,)), ((), ())), preferred_element_type=jnp.float32
    )


def stack_heads(src, which, dst):
    groups, _, own, _ = src.shape
    width = dst.shape[1]
    rows = groups * own
    for h in range(dst.shape[0] // rows):
        for y in range(groups):
            dst[pl.ds(h * rows + y * own, own), :] = src[y, which, :, pl.ds(h * width, width)]


def source(pos_ref, k, blocks):
    return lax.rem(pos_ref[0] + blocks - k, blocks)


def pack_kernel(q_ref, g_ref, trunk_ref, branch_ref, qg_ref, kv_ref, held, load_sems, sems):
    trunk = trunk_ref.shape[0]
    loads = [
        pltpu.make_async_copy(q_ref.at[0], held.at[0], load_sems.at[0]),
        pltpu.make_async_copy(g_ref.at[0], held.at[1], load_sems.at[1]),
        pltpu.make_async_copy(trunk_ref, kv_ref.at[pl.ds(0, trunk)], load_sems.at[2]),
        pltpu.make_async_copy(
            branch_ref.at[0], kv_ref.at[pl.ds(trunk, branch_ref.shape[1])], load_sems.at[3]
        ),
    ]
    for load in loads:
        load.start()
    stores = []
    for i in range(2):
        loads[i].wait()
        for y in range(qg_ref.shape[0]):
            stores.append(pltpu.make_async_copy(held.at[i], qg_ref.at[y, i], sems.at[y, i]))
            stores[-1].start()
    for load in loads[2:]:
        load.wait()
    for store in stores:
        store.wait()


def masks_kernel(nx, own, span, pos_ref, parent_ref, prefix_ref, lim_ref, reach_ref, closed):
    count = parent_ref.shape[1]
    lanes = lim_ref.shape[1]
    x, yh = pos_ref[0], pos_ref[2]
    above = lax.broadcasted_iota(jnp.int32, (count, count), 0)
    below = lax.broadcasted_iota(jnp.int32, (count, count), 1)
    reach = jnp.where((parent_ref[...] == above) | (above == below), 1.0, 0.0).astype(jnp.bfloat16)
    for _ in range(max(count - 1, 1).bit_length()):
        pairs = jnp.dot(reach, reach, preferred_element_type=jnp.float32)
        reach = jnp.minimum(pairs, 1.0).astype(jnp.bfloat16)
    closed[...] = reach.astype(jnp.float32)
    rows = count // nx
    lane = lax.broadcasted_iota(jnp.int32, (count, lanes), 1)
    row = lax.rem(lax.div(lane, own), rows // own) * (nx * own) + x * own + lax.rem(lane, own)
    chosen = jnp.where(lax.broadcasted_iota(jnp.int32, (count, lanes), 0) == row, 1.0, 0.0)
    chosen = chosen.astype(jnp.bfloat16)
    mine = closed[pl.ds(pl.multiple_of(yh * nx * own, nx * own), nx * own), :]
    reach_ref[...] = jnp.dot(mine.astype(jnp.bfloat16), chosen, preferred_element_type=jnp.float32)
    prefix = prefix_ref[...]
    part = lax.broadcasted_iota(jnp.int32, (TILE, count), 0)
    digits = jnp.where(part == 0, lax.div(prefix, 128), lax.rem(prefix, 128))
    digits = jnp.dot(
        digits.astype(jnp.float32).astype(jnp.bfloat16), chosen, preferred_element_type=jnp.float32
    )
    lim = (digits[0:1] * 128.0 + digits[1:2]).astype(jnp.int32)
    lim_ref[...] = lim - yh * span


def stats_kernel(shifts, last, pos_ref, lim_ref, reach_ref, *refs):
    count = len(shifts)
    if last:
        qs, gs, before_ref = refs[:3]
        kvs = refs[3 : 3 + count]
        after_ref, tops_ref, e_ref, s_ref = refs[3 + count :]
    else:
        qg_ref = refs[0]
        kvs = refs[1 : 1 + count]
        after_ref, tops_ref, e_ref, s_ref, qs, gs = refs[1 + count :]
        stack_heads(qg_ref, 0, qs)
        stack_heads(qg_ref, 1, gs)
    keys, wide = kvs[0].shape
    width = wide // 2
    lanes = qs.shape[0]
    scale = width ** (-0.5)
    trunk = keys - TILE
    power = scale * math.log2(math.e)
    ids = lax.broadcasted_iota(jnp.int32, (trunk, lanes), 0)
    if last:
        top, total, slope = (before_ref[i : i + 1, :] for i in range(3))
    else:
        top = jnp.full((1, lanes), MASKED, jnp.float32)
        total = jnp.zeros((1, lanes), jnp.float32)
        slope = jnp.zeros((1, lanes), jnp.float32)
    nows = []

    def score(i):
        b = source(pos_ref, shifts[i], 4)
        raw = dot_nt(kvs[i][:, :width], qs[...])
        near = jnp.where(ids < lim_ref[...] - b * trunk, raw[:trunk], MASKED)
        tree = jnp.where(
            reach_ref[pl.ds(pl.multiple_of(b * TILE, TILE), TILE), :] > 0.5, raw[trunk:], MASKED
        )
        e_ref[i, :trunk, :] = near
        e_ref[i, trunk:, :] = tree
        best = jnp.maximum(
            jnp.max(near, axis=0, keepdims=True), jnp.max(tree, axis=0, keepdims=True)
        )
        s_ref[i] = dot_nt(kvs[i][:, width:], gs[...])
        nows.append(jnp.maximum(nows[-1] if nows else top, best))
        tops_ref[pl.ds(i, 1), :] = nows[-1] * scale

    def weigh(i, total, slope):
        now = nows[i]
        fade = jnp.exp2(((nows[i - 1] if i else top) - now) * power)
        l = jnp.zeros((STRIP, lanes), jnp.float32)
        d = jnp.zeros((STRIP, lanes), jnp.float32)
        for t in range(keys // STRIP):
            at = pl.ds(t * STRIP, STRIP)
            p = jnp.exp2((e_ref[i, at, :] - now) * power)
            l = l + p
            d = d + p * s_ref[i, at, :]
            e_ref[i, at, :] = p
        return (
            total * fade + jnp.sum(l, axis=0, keepdims=True),
            slope * fade + jnp.sum(d, axis=0, keepdims=True),
        )

    for i in range(count):
        score(i)
    for i in range(count):
        total, slope = weigh(i, total, slope)
    top = nows[-1]
    if last:
        after_ref[0:1, :] = top * scale + jnp.log(total)
        after_ref[1:2, :] = slope / total
    else:
        after_ref[0:1, :] = top
        after_ref[1:2, :] = total
        after_ref[2:3, :] = slope


def grads_kernel(shifts, pos_ref, stats_ref, qs, gs, *refs):
    blocks = len(shifts[0]) + len(shifts[1])
    kvs = refs[6 : 6 + blocks]
    held = [
        (k, kvs[k], refs[3 * half].at[pl.ds(i, 1)], refs[3 * half + 1].at[i], refs[3 * half + 2].at[i])
        for half in range(2)
        for i, k in enumerate(shifts[half])
    ]
    qkeep_ref, qsend_ref, keep_ref, send_ref, tkeep_ref, tsend_ref = refs[6 + blocks : 12 + blocks]
    d_scr, p_scr, tree_d, tree_k, kv_scr, tree_scr, dq_scr, q_scr = refs[12 + blocks :]
    _, keys, lanes = d_scr.shape
    groups = stats_ref.shape[0]
    own = qkeep_ref.shape[1]
    rows = groups * own
    width = qs.shape[1]
    scale = width ** (-0.5)
    trunk = keys - TILE
    mine = pos_ref[1]
    q_low = lax.rem(pos_ref[2], 2)
    tree_low = lax.rem(pos_ref[0], 2)
    parts = [stats_ref[i, 0:1, :] for i in range(groups)]
    top = parts[0]
    for part in parts[1:]:
        top = jnp.maximum(top, part)
    total = jnp.zeros_like(top)
    for part in parts:
        total = total + jnp.exp(part - top)
    log_total = top + jnp.log(total)
    delta = jnp.zeros_like(top)
    for i in range(groups):
        delta = delta + jnp.exp(parts[i] - log_total) * stats_ref[i, 1:2, :]

    def slopes_of(step):
        _, _, top_ref, e_ref, s_ref = held[step]
        fade = jnp.exp(top_ref[...] - log_total)
        for t in range(keys // TILE):
            at = pl.ds(t * TILE, TILE)
            p = e_ref[at, :] * fade
            d_scr[step % 2, at, :] = (p * (s_ref[at, :] - delta)).astype(jnp.bfloat16)
            p_scr[step % 2, at, :] = p.astype(jnp.bfloat16)

    def products(step):
        k, kv_ref, _, _, _ = held[step]
        b = source(pos_ref, k, blocks)
        slot = step % 2
        dk = scale * jnp.dot(d_scr[slot], qs[...], preferred_element_type=jnp.float32)
        dv = jnp.dot(p_scr[slot], gs[...], preferred_element_type=jnp.float32)
        for half, grad in enumerate((dk, dv)):
            at = pl.ds(half * width, width)
            for piece in range(trunk // TILE):
                kv_scr[slot, piece % 2, piece // 2, :, at] = grad[piece * TILE : (piece + 1) * TILE]
            tree_scr[lax.div(b, 2), lax.rem(b, 2), :, at] = grad[trunk:]
        keep_ref[b] = kv_scr[slot, mine]
        send_ref[b] = kv_scr[slot, 1 - mine].astype(jnp.bfloat16)
        tree = pl.ds(step * TILE, TILE)
        tree_k[tree, :] = kv_ref[trunk:, :width]
        tree_d[tree, :] = d_scr[slot, trunk:, :]
        part = dot_tn(kv_ref[:trunk, :width], d_scr[slot, :trunk, :])
        if step == blocks - 1:
            part += dot_tn(tree_k[...], tree_d[...])
        if step == 0:
            dq_scr[...] = part
        else:
            dq_scr[...] += part

    slopes_of(0)
    for step in range(blocks):
        if step + 1 < blocks:
            slopes_of(step + 1)
        products(step)
    for h in range(lanes // rows):
        piece = (scale * dq_scr[:, pl.ds(h * rows, rows)]).T
        q_scr[:, :, :, pl.ds(h * width, width)] = piece.reshape(groups // 2, 2, own, width)
    qkeep_ref[...] = q_scr[:, q_low]
    qsend_ref[...] = q_scr[:, 1 - q_low].astype(jnp.bfloat16)
    tkeep_ref[...] = tree_scr[:, tree_low]
    tsend_ref[...] = tree_scr[:, 1 - tree_low]


def grads_scratch(keys, lanes, width, nx, ny, own):
    bf16 = jnp.bfloat16
    return [
        pltpu.VMEM((2, keys, lanes), bf16),
        pltpu.VMEM((2, keys, lanes), bf16),
        pltpu.VMEM((nx * TILE, lanes), bf16),
        pltpu.VMEM((nx * TILE, width), bf16),
        pltpu.VMEM((2, 2, (keys - TILE) // (2 * own), own, 2 * width), jnp.float32),
        pltpu.VMEM((nx // 2, 2, own, 2 * width), jnp.float32),
        pltpu.VMEM((width, lanes), jnp.float32),
        pltpu.VMEM((ny // 2, 2, own, width * lanes // (ny * own)), jnp.float32),
    ]


def swap(x, axis):
    return lax.all_to_all(x, axis, 0, 0)


def spread(x, axis):
    return swap(jnp.broadcast_to(x[None], (lax.axis_size(axis),) + x.shape), axis)


def turn(x, axis, k):
    n = lax.axis_size(axis)
    return lax.ppermute(x, axis, [(i, (i + k) % n) for i in range(n)])


def meet(x, axis, bit):
    return lax.ppermute(x, axis, [(i, i ^ bit) for i in range(lax.axis_size(axis))])


def pick(x, which):
    return lax.dynamic_index_in_dim(x, which, 0, keepdims=False)


def per_device(queries, out_grad, branch_kv, trunk_kv, parent, prefix):
    bf16, f32 = jnp.bfloat16, jnp.float32
    width = trunk_kv.shape[1] // 2
    own = queries.shape[1]
    heads = queries.shape[2] // width
    nx, ny = lax.axis_size("x"), lax.axis_size("yh")
    x, yh, core = lax.axis_index("x"), lax.axis_index("yh"), lax.axis_index("c")
    span = trunk_kv.shape[0] * nx
    rows = own * ny
    lanes = rows * heads
    pos = jnp.stack([x, core, yh])

    shape = jax.ShapeDtypeStruct
    vmem = pl.BlockSpec(memory_space=pltpu.VMEM)
    smem = pl.BlockSpec(memory_space=pltpu.SMEM)
    anywhere = pl.BlockSpec(memory_space=pl.ANY)
    qg, kv = pl.pallas_call(
        pack_kernel,
        out_shape=(
            shape((ny, 2) + queries.shape[1:], bf16),
            shape((trunk_kv.shape[0] + own, 2 * width), bf16),
        ),
        in_specs=[anywhere] * 4,
        out_specs=(anywhere, vmem),
        scratch_shapes=[
            pltpu.VMEM((2,) + queries.shape[1:], bf16),
            pltpu.SemaphoreType.DMA((4,)),
            pltpu.SemaphoreType.DMA((ny, 2)),
        ],
        name="pack",
    )(queries, out_grad, trunk_kv, branch_kv)
    qg = swap(qg, "yh")
    kvs = [turn(kv, "x", k) for k in range(1, nx)]
    kvs = [jnp.concatenate([trunk_kv, branch_kv[0]], axis=0)] + kvs
    shifts = ((0, 1), (2, 3))

    lim, reach = pl.pallas_call(
        functools.partial(masks_kernel, nx, own, span),
        out_shape=(shape((1, lanes), jnp.int32), shape((nx * own, lanes), f32)),
        in_specs=[smem, vmem, vmem],
        out_specs=(vmem, vmem),
        scratch_shapes=[pltpu.VMEM((parent.shape[1], parent.shape[1]), f32)],
        compiler_params=pltpu.CompilerParams(vmem_limit_bytes=4 << 20),
        name="masks",
    )(pos, parent, prefix)
    keys = kv.shape[0]
    head = (pos, lim, reach)
    rest = [qg]
    held = []
    for half in range(2):
        count = len(shifts[half])
        outs = [
            shape((3 - half, lanes), f32),
            shape((count, lanes), f32),
            shape((count, keys, lanes), f32),
            shape((count, keys, lanes), f32),
        ]
        if half == 0:
            outs += [shape((lanes, width), bf16)] * 2
        stats, tops, e, s, *stacked = pl.pallas_call(
            functools.partial(stats_kernel, shifts[half], half == 1),
            out_shape=tuple(outs),
            in_specs=[smem] + [vmem] * (2 + len(rest) + count),
            out_specs=(vmem,) * len(outs),
            compiler_params=pltpu.CompilerParams(vmem_limit_bytes=6 << 20),
            name="stats",
        )(*head, *rest, *[kvs[k] for k in shifts[half]])
        held += [tops, e, s]
        if half == 0:
            qs, gs = stacked
            rest = [qs, gs, stats]
    stats = spread(stats, "yh")
    pieces = trunk_kv.shape[0] // (2 * own)
    q_keep, q_send, keep, send, t_keep, t_send = pl.pallas_call(
        functools.partial(grads_kernel, shifts),
        out_shape=(
            shape((ny // 2, own, heads * width), f32),
            shape((ny // 2, own, heads * width), bf16),
            shape((nx, pieces, own, 2 * width), f32),
            shape((nx, pieces, own, 2 * width), bf16),
            shape((nx // 2, own, 2 * width), f32),
            shape((nx // 2, own, 2 * width), f32),
        ),
        in_specs=[smem] + [vmem] * (9 + nx),
        out_specs=(vmem,) * 6,
        scratch_shapes=grads_scratch(keys, lanes, width, nx, ny, own),
        compiler_params=pltpu.CompilerParams(vmem_limit_bytes=12 << 20),
        name="grads",
    )(pos, stats, qs, gs, *held, *kvs)
    other = turn(send, "c", 1)
    trunk = (keep + other.astype(f32)).astype(bf16).reshape(nx * pieces, own, 2 * width)
    trunk = swap(trunk, ("x", "z", "yl"))
    high = lax.div(yh, 2)
    part = q_keep + meet(q_send, "yh", 1).astype(f32)
    query_grad = pick(part, high) + meet(pick(part, 1 - high).astype(bf16), "yh", 2).astype(f32)
    query_grad = query_grad.astype(bf16)
    high = lax.div(x, 2)
    part = t_keep + meet(t_send, "x", 1)
    branch = pick(part, high) + meet(pick(part, 1 - high), "x", 2)
    trunk = jnp.sum(trunk.astype(f32), axis=0)
    return (query_grad[None], branch[None], trunk)


def solution(mesh):
    fine = Mesh(mesh.devices.reshape(4, 4, 8, 2, 2), ("yh", "x") + SET)
    ctx = ("yh", "x")
    return jax.shard_map(
        per_device,
        mesh=fine,
        in_specs=(
            P(SET, ctx, None),
            P(SET, ctx, None),
            P(SET, ctx, None),
            P(ctx, None),
            P(SET, None),
            P(SET, None),
        ),
        out_specs=(P(SET, ctx, None), P(SET, ctx, None), P(ctx + SET, None)),
        check_vma=False,
    )
```

time: 106 us -> 95 us (0.90)
  waiting for transfers between devices: 26.6 us -> 14.2 us
  starting transfers between devices: 40.6 us -> 45.1 us
  Pallas kernels: 17.9 us -> 14.4 us
  blocking collectives: 11.7 us -> 14.6 us
  matrix products: 2.65 us -> 0 us
  other arithmetic: 2.22 us -> 4.02 us
  local copies, waits for them, and re-layouts: 2.5 us -> 1.39 us
    all_to_all x3 -> x2, waiting for transfers between devices: 17.5 us -> 4.84 us  [swap(): return lax.all_to_all(x, axis, 0, 0)]
    ppermute x2 -> x4, starting transfers between devices: 7.52 us -> 12.3 us  [meet(): lax.ppermute(x, axis, [(i, i ^ bit) for i in range(lax.axis_size(axis))])]
    pallas_call x2, Pallas kernels: 9.17 us -> 5.43 us  [per_device(): pl.pallas_call(functools.partial(stats_kernel, shifts[half], half == 1),...]
    all_to_all x1, blocking collectives: 11.7 us -> 14.6 us  [swap(): return lax.all_to_all(x, axis, 0, 0)]
    dot_general x4 -> x0, matrix products: 2.65 us -> none  [ancestors_t(): jnp.dot(reach, reach, preferred_element_type=jnp.float32)]
    ppermute x3 -> x4, waiting for transfers between devices: 0.01 us -> 2.41 us  [turn(): return lax.ppermute(x, axis, [(i, (i + k) % n) for i in range(n)])]
    pallas_call x0 -> x1, Pallas kernels: none -> 2.34 us  [per_device(): pl.pallas_call(functools.partial(masks_kernel, nx, own, span), out_shape=...]
    pallas_call x1, Pallas kernels: 6.27 us -> 4.16 us  [per_device(): pl.pallas_call(functools.partial(grads_kernel, shifts), out_shape=(shape(...]
  transfers between devices with their start and end apart: 8 -> 10, of which waited for: 3 -> 4; matrix products, arithmetic and copies ran while one was open for 6% -> 4% of each run, Pallas kernels for 4% -> 5%
where the time goes in v3:
time: 95 us; the launch traced here: 94.5 us
  starting transfers between devices  45.1 us (47%)
  blocking collectives  14.6 us (15%)
  Pallas kernels  14.4 us (15%)
  waiting for transfers between devices  14.2 us (15%)
  other arithmetic  4.02 us (4%)
  local copies, waits for them, and re-layouts  1.39 us (1%)
    all_to_all x2, starting transfers between devices, swap(): return lax.all_to_all(x, axis, 0, 0)  20.3 us
    all_to_all x1, blocking collectives, swap(): return lax.all_to_all(x, axis, 0, 0)  14.6 us
    ppermute x4, starting transfers between devices, turn(): return lax.ppermute(x, axis, [(i, (i + k) % n) for i in range(n)])  12.4 us
    ppermute x4, starting transfers between devices, meet(): lax.ppermute(x, axis, [(i, i ^ bit) for i in range(lax.axis_size(axis))])  12.3 us
    ppermute x4, waiting for transfers between devices, meet(): lax.ppermute(x, axis, [(i, i ^ bit) for i in range(lax.axis_size(axis))])  6.95 us
    pallas_call x2, Pallas kernels, per_device(): pl.pallas_call(functools.partial(stats_kernel, shifts[half], half == 1),...  5.43 us
    all_to_all x2, waiting for transfers between devices, swap(): return lax.all_to_all(x, axis, 0, 0)  4.84 us
    pallas_call x1, Pallas kernels, per_device(): pl.pallas_call(functools.partial(grads_kernel, shifts), out_shape=(shape(...  4.16 us
  transfers between devices with their start and end apart: 10, of which 4 were waited for; matrix products, arithmetic and copies ran while one was open for 4% of the time, Pallas kernels for 5%

profile of v3, /device:TPU:2, one launch (start us, length us, event | category | flops | bytes accessed | tf_op | source)
XLA Modules:
  0.0 94.5 jit_solution(4081169120825683349)
XLA Ops:
  0.6 2.4 %pack.1 = (bf16[4,2,16,2048]{3,2,1,0:T(8,128)(2,1)}, bf16[528,256]{1,0:T(8,128)(2,1)}) custom-call(bf16[1,16,2048]{2,1,0:T(8,128)(2,1)} %q_ref.1, bf16[1,16,2048]{2,1,0:T(8,128)(2,1)} %g_ref.1, bf16[512,256]{1,0:T(8,128)(2,1)} %trunk_ref.1, bf16[1,16,256]{2,1,0:T(8,128)(2,1)} %branch_ref.1), custom_call_target="tpu_custom_call" | custom-call | tf_op jit(solution)/shard_map/pack/pallas_call | solution.py:298
  3.1 7.1 %all-to-all-start = ((bf16[4,2,16,2048]{3,2,1,0:T(8,128)(2,1)}), bf16[4,2,16,2048]{3,2,1,0:T(8,128)(2,1)S(1)}, u32[]{:S(2)}, u32[]{:S(2)}) async-start(bf16[4,2,16,2048]{3,2,1,0:T(8,128)(2,1)} %get-tuple-element.25), calls=%async_computation | async-start | bytes 1048576 | tf_op jit(solution)/shard_map/all_to_all | solution.py:262
  10.2 3.4 %collective-permute-start = (bf16[528,256]{1,0:T(8,128)(2,1)}, bf16[528,256]{1,0:T(8,128)(2,1)S(1)}, u32[]{:S(2)}, u32[]{:S(2)}) collective-permute-start(bf16[528,256]{1,0:T(8,128)(2,1)} %get-tuple-element.26), channel_id=1, source_target_pairs={{0,32},{32,64},{64,96},{96,0},{1,33},{33,65},{65,97},{97,1},{2,34}... | collective-permute-start | bytes 811016 | tf_op jit(solution)/shard_map/ppermute | solution.py:271
  13.6 4.8 %collective-permute-start.1 = (bf16[528,256]{1,0:T(8,128)(2,1)}, bf16[528,256]{1,0:T(8,128)(2,1)S(1)}, u32[]{:S(2)}, u32[]{:S(2)}) collective-permute-start(bf16[528,256]{1,0:T(8,128)(2,1)} %get-tuple-element.26), channel_id=1, source_target_pairs={{0,64},{32,96},{64,0},{96,32},{1,65},{33,97},{65,1},{97,33},{2,66}... | collective-permute-start | bytes 811016 | tf_op jit(solution)/shard_map/ppermute | solution.py:271
  18.4 2.3 %collective-permute-start.2 = (bf16[528,256]{1,0:T(8,128)(2,1)}, bf16[528,256]{1,0:T(8,128)(2,1)S(1)}, u32[]{:S(2)}, u32[]{:S(2)}) collective-permute-start(bf16[528,256]{1,0:T(8,128)(2,1)} %get-tuple-element.26), channel_id=1, source_target_pairs={{0,96},{32,0},{64,32},{96,64},{1,97},{33,1},{65,33},{97,65},{2,98}... | collective-permute-start | bytes 811016 | tf_op jit(solution)/shard_map/ppermute | solution.py:271
  20.7 0.1 pad_add_fusion.pos_ref
  20.8 0.0 copy-start
  20.8 0.7 copy-done
  21.4 0.0 copy-start.1
  21.4 0.7 copy-done.1
  22.1 2.3 %masks.1 = (s32[1,1024]{1,0:T(1,128)S(1)}, f32[64,1024]{1,0:T(8,128)S(1)}) custom-call(s32[3]{0:T(128)S(1)} %pad_add_fusion.pos_ref, s32[1,256]{1,0:T(1,128)S(1)} %copy-done, s32[1,256]{1,0:T(1,128)S(1)} %copy-done.1), custom_call_target="tpu_custom_call" | custom-call | tf_op jit(solution)/shard_map/masks/pallas_call | solution.py:318
  24.5 1.0 %pad_maximum_fusion.refs_1_.refs_6_ = bf16[528,256]{1,0:T(8,128)(2,1)S(1)} fusion(bf16[16,256]{1,0:T(8,128)(2,1)} %bitcast.23, bf16[512,256]{1,0:T(8,128)(2,1)} %trunk_ref.1), kind=kLoop, calls=%fused_computation.2 | loop fusion | flops 540672 | bytes 540672 | tf_op jit(solution)/shard_map/concatenate | solution.py:315
  25.5 0.0 collective-permute-done.refs_2_.refs_7_
  25.5 0.0 all-to-all-done.refs_0_
  25.5 2.7 %stats.2 = (f32[3,1024]{1,0:T(4,128)S(1)}, f32[2,1024]{1,0:T(2,128)S(1)}, f32[2,528,1024]{2,1,0:T(8,128)S(1)}, f32[2,528,1024]{2,1,0:T(8,128)S(1)}, bf16[1024,12...) custom-call(s32[3]{0:T(128)S(1)} %pad_add_fusion.pos_ref, s32[1,1024]{1,0:T(1,128)S(1)} %get-tuple-element.23.lim_ref, ...), custom_call_target="tpu_custom_call" | custom-call | tf_op jit(solution)/shard_map/stats/pallas_call | solution.py:341
  28.2 0.0 collective-permute-done.1.refs_3_.refs_8_
  28.2 2.4 %collective-permute-done.2.refs_4_.refs_9_ = bf16[528,256]{1,0:T(8,128)(2,1)S(1)} collective-permute-done((bf16[528,256]{1,0:T(8,128)(2,1)}, bf16[528,256]{1,0:T(8,128)(2,1)S(1)}, u32[]{:S(2)}, u32[]{:S(2)}) %collective-permute-start.2) | collective-permute-done | bytes 270368 | tf_op jit(solution)/shard_map/ppermute | solution.py:271
  30.6 2.7 %stats.3 = (f32[2,1024]{1,0:T(2,128)S(1)}, f32[2,1024]{1,0:T(2,128)S(1)}, f32[2,528,1024]{2,1,0:T(8,128)S(1)}, f32[2,528,1024]{2,1,0:T(8,128)S(1)}) custom-call(s32[3]{0:T(128)S(1)} %pad_add_fusion.pos_ref, s32[1,1024]{1,0:T(1,128)S(1)} %get-tuple-element.23.lim_ref, f32[64,1024]{1,0:T(8,128)S(1)} %get-tuple-element.24.reach_ref, ...), custom_call_target="tpu_custom_call" | custom-call | tf_op jit(solution)/shard_map/stats/pallas_call | solution.py:341
  33.4 14.6 %all_to_all.15.stats_ref = f32[4,2,1024]{2,1,0:T(2,128)S(1)} all-to-all(f32[4,2,1024]{2,1,0:T(2,128)S(1)} %broadcast_in_dim.12), channel_id=1, replica_groups=mesh['yh'=4,'x'=4,'z'=8,'yl'=2,'c'=2] {'yh'}, dimensions={0} | all-to-all | bytes 65536 | tf_op jit(solution)/shard_map/all_to_all | solution.py:262
  47.9 4.2 %grads.1 = (f32[2,16,2048]{2,1,0:T(8,128)S(1)}, bf16[2,16,2048]{2,1,0:T(8,128)(2,1)S(1)}, f32[4,16,16,256]{3,2,1,0:T(8,128)S(1)}, bf16[4,16,16,256]{3,2,1,0:T(8,...) custom-call(s32[3]{0:T(128)S(1)} %pad_add_fusion.pos_ref, f32[4,2,1024]{2,1,0:T(2,128)S(1)} %all_to_all.15.stats_ref, ...), custom_call_target="tpu_custom_call" | custom-call | tf_op jit(solution)/shard_map/grads/pallas_call | solution.py:355
  52.1 1.9 %collective-permute-start.7 = (bf16[4,16,16,256]{3,2,1,0:T(8,128)(2,1)S(1)}, bf16[4,16,16,256]{3,2,1,0:T(8,128)(2,1)S(1)}, u32[]{:S(2)}, u32[]{:S(2)}) collective-permute-start(bf16[4,16,16,256]{3,2,1,0:T(8,128)(2,1)S(1)} %get-tuple-element.42), channel_id=1, source_target_pairs={{0,1},{1,0},{2,3},{3,2},{4,5},{5,4},{6,7},{7,6},{8,9},{9,8},{10,11... | collective-permute-start | bytes 1572872 | tf_op jit(solution)/shard_map/ppermute | solution.py:271
  54.0 2.3 %collective-permute-start.5 = (f32[2,16,256]{2,1,0:T(8,128)S(1)}, f32[2,16,256]{2,1,0:T(8,128)S(1)}, u32[]{:S(2)}, u32[]{:S(2)}) collective-permute-start(f32[2,16,256]{2,1,0:T(8,128)S(1)} %get-tuple-element.40), channel_id=1, source_target_pairs={{0,32},{32,0},{64,96},{96,64},{1,33},{33,1},{65,97},{97,65},{2,34}... | collective-permute-start | bytes 98312 | tf_op jit(solution)/shard_map/ppermute | solution.py:275
  56.4 2.5 %collective-permute-start.3 = (bf16[2,16,2048]{2,1,0:T(8,128)(2,1)S(1)}, bf16[2,16,2048]{2,1,0:T(8,128)(2,1)S(1)}, u32[]{:S(2)}, u32[]{:S(2)}) collective-permute-start(bf16[2,16,2048]{2,1,0:T(8,128)(2,1)S(1)} %get-tuple-element.38), channel_id=1, source_target_pairs={{0,128},{128,0},{256,384},{384,256},{1,129},{129,1},{257,385},{385... | collective-permute-start | bytes 393224 | tf_op jit(solution)/shard_map/ppermute | solution.py:275
  58.8 1.0 %collective-permute-done.5 = f32[2,16,256]{2,1,0:T(8,128)S(1)} collective-permute-done((f32[2,16,256]{2,1,0:T(8,128)S(1)}, f32[2,16,256]{2,1,0:T(8,128)S(1)}, u32[]{:S(2)}, u32[]{:S(2)}) %collective-permute-start.5) | collective-permute-done | bytes 32800 | tf_op jit(solution)/shard_map/ppermute | solution.py:275
  59.9 3.8 %collective-permute-start.6 = (f32[16,256]{1,0:T(8,128)S(1)}, f32[16,256]{1,0:T(8,128)S(1)}, u32[]{:S(2)}, u32[]{:S(2)}) collective-permute-start(f32[16,256]{1,0:T(8,128)S(1)} %dynamic-slice_bitcast_fusion), channel_id=1, source_target_pairs={{0,64},{32,96},{64,0},{96,32},{1,65},{33,97},{65,1},{97,33},{2,66}... | collective-permute-start | bytes 49160 | tf_op jit(solution)/shard_map/ppermute | solution.py:275
  63.7 0.0 collective-permute-done.7
  63.7 1.0 %add_convert_fusion = bf16[4,16,16,256]{3,2,1,0:T(8,128)(2,1)} fusion(f32[4,16,16,256]{3,2,1,0:T(8,128)S(1)} %get-tuple-element.41, bf16[4,16,16,256]{3,2,1,0:T(8,128)(2,1)S(1)} %collective-permute-done.7), kind=kLoop, calls=%fused_computation.1 | loop fusion | flops 786432 | bytes 2097152 | tf_op jit(solution)/shard_map/convert_element_type | solution.py:372
  64.6 13.2 %all-to-all-start.2 = ((bf16[64,16,256]{2,1,0:T(8,128)(2,1)}), bf16[64,16,256]{2,1,0:T(8,128)(2,1)S(1)}, u32[]{:S(2)}, u32[]{:S(2)}) async-start(bf16[64,16,256]{2,1,0:T(8,128)(2,1)} %bitcast.10), calls=%async_computation.2 | async-start | bytes 1048576 | tf_op jit(solution)/shard_map/all_to_all | solution.py:262
  77.9 0.0 collective-permute-done.3
  77.9 3.8 %collective-permute-start.4 = (bf16[16,2048]{1,0:T(8,128)(2,1)S(1)}, bf16[16,2048]{1,0:T(8,128)(2,1)S(1)}, u32[]{:S(2)}, u32[]{:S(2)}) collective-permute-start(bf16[16,2048]{1,0:T(8,128)(2,1)S(1)} %fusion.1), channel_id=1, source_target_pairs={{0,256},{128,384},{256,0},{384,128},{1,257},{129,385},{257,1},{385... | collective-permute-start | bytes 196616 | tf_op jit(solution)/shard_map/ppermute | solution.py:275
  81.7 0.0 collective-permute-done.6
  81.7 0.6 fusion.3
  82.4 5.9 %collective-permute-done.4 = bf16[16,2048]{1,0:T(8,128)(2,1)S(1)} collective-permute-done((bf16[16,2048]{1,0:T(8,128)(2,1)S(1)}, bf16[16,2048]{1,0:T(8,128)(2,1)S(1)}, u32[]{:S(2)}, u32[]{:S(2)}) %collective-permute-start.4) | collective-permute-done | bytes 65568 | tf_op jit(solution)/shard_map/ppermute | solution.py:275
  88.3 0.6 fusion.2
  88.9 4.8 %all-to-all-done.2 = bf16[64,16,256]{2,1,0:T(8,128)(2,1)S(1)} async-done(((bf16[64,16,256]{2,1,0:T(8,128)(2,1)}), bf16[64,16,256]{2,1,0:T(8,128)(2,1)S(1)}, u32[]{:S(2)}, u32[]{:S(2)}) %all-to-all-start.2) | async-done | bytes 524320 | tf_op jit(solution)/shard_map/all_to_all | solution.py:262
  93.8 0.7 convert_reduce_fusion
  (5 shorter events, 0.1 us)
Async XLA Ops:
  3.1 22.4 %all-to-all-start = ((bf16[4,2,16,2048]{3,2,1,0:T(8,128)(2,1)}), bf16[4,2,16,2048]{3,2,1,0:T(8,128)(2,1)S(1)}, u32[]{:S(2)}, u32[]{:S(2)}) async-start(bf16[4,2,16,2048]{3,2,1,0:T(8,128)(2,1)} %get-tuple-element.25), calls=%async_computation | async-start | bytes 1048576 | tf_op jit(solution)/shard_map/all_to_all | solution.py:262
  10.2 15.3 %collective-permute-start = (bf16[528,256]{1,0:T(8,128)(2,1)}, bf16[528,256]{1,0:T(8,128)(2,1)S(1)}, u32[]{:S(2)}, u32[]{:S(2)}) collective-permute-start(bf16[528,256]{1,0:T(8,128)(2,1)} %get-tuple-element.26), channel_id=1, source_target_pairs={{0,32},{32,64},{64,96},{96,0},{1,33},{33,65},{65,97},{97,1},{2,34}... | collective-permute-start | bytes 811016 | tf_op jit(solution)/shard_map/ppermute | solution.py:271
  13.6 14.6 %collective-permute-start.1 = (bf16[528,256]{1,0:T(8,128)(2,1)}, bf16[528,256]{1,0:T(8,128)(2,1)S(1)}, u32[]{:S(2)}, u32[]{:S(2)}) collective-permute-start(bf16[528,256]{1,0:T(8,128)(2,1)} %get-tuple-element.26), channel_id=1, source_target_pairs={{0,64},{32,96},{64,0},{96,32},{1,65},{33,97},{65,1},{97,33},{2,66}... | collective-permute-start | bytes 811016 | tf_op jit(solution)/shard_map/ppermute | solution.py:271
  18.4 12.3 %collective-permute-start.2 = (bf16[528,256]{1,0:T(8,128)(2,1)}, bf16[528,256]{1,0:T(8,128)(2,1)S(1)}, u32[]{:S(2)}, u32[]{:S(2)}) collective-permute-start(bf16[528,256]{1,0:T(8,128)(2,1)} %get-tuple-element.26), channel_id=1, source_target_pairs={{0,96},{32,0},{64,32},{96,64},{1,97},{33,1},{65,33},{97,65},{2,98}... | collective-permute-start | bytes 811016 | tf_op jit(solution)/shard_map/ppermute | solution.py:271
  20.8 0.7 copy-start
  21.4 0.7 copy-start.1
  52.1 11.6 %collective-permute-start.7 = (bf16[4,16,16,256]{3,2,1,0:T(8,128)(2,1)S(1)}, bf16[4,16,16,256]{3,2,1,0:T(8,128)(2,1)S(1)}, u32[]{:S(2)}, u32[]{:S(2)}) collective-permute-start(bf16[4,16,16,256]{3,2,1,0:T(8,128)(2,1)S(1)} %get-tuple-element.42), channel_id=1, source_target_pairs={{0,1},{1,0},{2,3},{3,2},{4,5},{5,4},{6,7},{7,6},{8,9},{9,8},{10,11... | collective-permute-start | bytes 1572872 | tf_op jit(solution)/shard_map/ppermute | solution.py:271
  54.0 5.8 %collective-permute-start.5 = (f32[2,16,256]{2,1,0:T(8,128)S(1)}, f32[2,16,256]{2,1,0:T(8,128)S(1)}, u32[]{:S(2)}, u32[]{:S(2)}) collective-permute-start(f32[2,16,256]{2,1,0:T(8,128)S(1)} %get-tuple-element.40), channel_id=1, source_target_pairs={{0,32},{32,0},{64,96},{96,64},{1,33},{33,1},{65,97},{97,65},{2,34}... | collective-permute-start | bytes 98312 | tf_op jit(solution)/shard_map/ppermute | solution.py:275
  56.4 21.5 %collective-permute-start.3 = (bf16[2,16,2048]{2,1,0:T(8,128)(2,1)S(1)}, bf16[2,16,2048]{2,1,0:T(8,128)(2,1)S(1)}, u32[]{:S(2)}, u32[]{:S(2)}) collective-permute-start(bf16[2,16,2048]{2,1,0:T(8,128)(2,1)S(1)} %get-tuple-element.38), channel_id=1, source_target_pairs={{0,128},{128,0},{256,384},{384,256},{1,129},{129,1},{257,385},{385... | collective-permute-start | bytes 393224 | tf_op jit(solution)/shard_map/ppermute | solution.py:275
  59.9 21.9 %collective-permute-start.6 = (f32[16,256]{1,0:T(8,128)S(1)}, f32[16,256]{1,0:T(8,128)S(1)}, u32[]{:S(2)}, u32[]{:S(2)}) collective-permute-start(f32[16,256]{1,0:T(8,128)S(1)} %dynamic-slice_bitcast_fusion), channel_id=1, source_target_pairs={{0,64},{32,96},{64,0},{96,32},{1,65},{33,97},{65,1},{97,33},{2,66}... | collective-permute-start | bytes 49160 | tf_op jit(solution)/shard_map/ppermute | solution.py:275
  64.6 29.1 %all-to-all-start.2 = ((bf16[64,16,256]{2,1,0:T(8,128)(2,1)}), bf16[64,16,256]{2,1,0:T(8,128)(2,1)S(1)}, u32[]{:S(2)}, u32[]{:S(2)}) async-start(bf16[64,16,256]{2,1,0:T(8,128)(2,1)} %bitcast.10), calls=%async_computation.2 | async-start | bytes 1048576 | tf_op jit(solution)/shard_map/all_to_all | solution.py:262
  77.9 10.3 %collective-permute-start.4 = (bf16[16,2048]{1,0:T(8,128)(2,1)S(1)}, bf16[16,2048]{1,0:T(8,128)(2,1)S(1)}, u32[]{:S(2)}, u32[]{:S(2)}) collective-permute-start(bf16[16,2048]{1,0:T(8,128)(2,1)S(1)} %fusion.1), channel_id=1, source_target_pairs={{0,256},{128,384},{256,0},{384,128},{1,257},{129,385},{257,1},{385... | collective-permute-start | bytes 196616 | tf_op jit(solution)/shard_map/ppermute | solution.py:275

commit v4 on v3

--- a/solution.py
+++ b/solution.py
@@ -40,37 +40,13 @@
     return lax.rem(pos_ref[0] + blocks - k, blocks)
 
 
-def pack_kernel(q_ref, g_ref, trunk_ref, branch_ref, qg_ref, kv_ref, held, load_sems, sems):
-    trunk = trunk_ref.shape[0]
-    loads = [
-        pltpu.make_async_copy(q_ref.at[0], held.at[0], load_sems.at[0]),
-        pltpu.make_async_copy(g_ref.at[0], held.at[1], load_sems.at[1]),
-        pltpu.make_async_copy(trunk_ref, kv_ref.at[pl.ds(0, trunk)], load_sems.at[2]),
-        pltpu.make_async_copy(
-            branch_ref.at[0], kv_ref.at[pl.ds(trunk, branch_ref.shape[1])], load_sems.at[3]
-        ),
-    ]
-    for load in loads:
-        load.start()
-    stores = []
-    for i in range(2):
-        loads[i].wait()
-        for y in range(qg_ref.shape[0]):
-            stores.append(pltpu.make_async_copy(held.at[i], qg_ref.at[y, i], sems.at[y, i]))
-            stores[-1].start()
-    for load in loads[2:]:
-        load.wait()
-    for store in stores:
-        store.wait()
-
-
-def masks_kernel(nx, own, span, pos_ref, parent_ref, prefix_ref, lim_ref, reach_ref, closed):
-    count = parent_ref.shape[1]
+def masks_kernel(nx, own, span, pos_ref, trees_ref, lim_ref, reach_ref, closed):
+    count = trees_ref.shape[1]
     lanes = lim_ref.shape[1]
     x, yh = pos_ref[0], pos_ref[2]
     above = lax.broadcasted_iota(jnp.int32, (count, count), 0)
     below = lax.broadcasted_iota(jnp.int32, (count, count), 1)
-    reach = jnp.where((parent_ref[...] == above) | (above == below), 1.0, 0.0).astype(jnp.bfloat16)
+    reach = jnp.where((trees_ref[0:1, :] == above) | (above == below), 1.0, 0.0).astype(jnp.bfloat16)
     for _ in range(max(count - 1, 1).bit_length()):
         pairs = jnp.dot(reach, reach, preferred_element_type=jnp.float32)
         reach = jnp.minimum(pairs, 1.0).astype(jnp.bfloat16)
@@ -82,7 +58,7 @@
     chosen = chosen.astype(jnp.bfloat16)
     mine = closed[pl.ds(pl.multiple_of(yh * nx * own, nx * own), nx * own), :]
     reach_ref[...] = jnp.dot(mine.astype(jnp.bfloat16), chosen, preferred_element_type=jnp.float32)
-    prefix = prefix_ref[...]
+    prefix = trees_ref[1:2, :]
     part = lax.broadcasted_iota(jnp.int32, (TILE, count), 0)
     digits = jnp.where(part == 0, lax.div(prefix, 128), lax.rem(prefix, 128))
     digits = jnp.dot(
@@ -294,36 +270,22 @@
     shape = jax.ShapeDtypeStruct
     vmem = pl.BlockSpec(memory_space=pltpu.VMEM)
     smem = pl.BlockSpec(memory_space=pltpu.SMEM)
-    anywhere = pl.BlockSpec(memory_space=pl.ANY)
-    qg, kv = pl.pallas_call(
-        pack_kernel,
-        out_shape=(
-            shape((ny, 2) + queries.shape[1:], bf16),
-            shape((trunk_kv.shape[0] + own, 2 * width), bf16),
-        ),
-        in_specs=[anywhere] * 4,
-        out_specs=(anywhere, vmem),
-        scratch_shapes=[
-            pltpu.VMEM((2,) + queries.shape[1:], bf16),
-            pltpu.SemaphoreType.DMA((4,)),
-            pltpu.SemaphoreType.DMA((ny, 2)),
-        ],
-        name="pack",
-    )(queries, out_grad, trunk_kv, branch_kv)
-    qg = swap(qg, "yh")
-    kvs = [turn(kv, "x", k) for k in range(1, nx)]
-    kvs = [jnp.concatenate([trunk_kv, branch_kv[0]], axis=0)] + kvs
+    qg = spread(jnp.stack([queries[0], out_grad[0]]), "yh")
+    kv = jnp.concatenate([trunk_kv, branch_kv[0]], axis=0)
+    kvs = [kv] + [None] * (nx - 1)
+    for k in range(1, nx):
+        kvs[k] = turn(kv, "x", k)
     shifts = ((0, 1), (2, 3))
 
     lim, reach = pl.pallas_call(
         functools.partial(masks_kernel, nx, own, span),
         out_shape=(shape((1, lanes), jnp.int32), shape((nx * own, lanes), f32)),
-        in_specs=[smem, vmem, vmem],
+        in_specs=[smem, vmem],
         out_specs=(vmem, vmem),
         scratch_shapes=[pltpu.VMEM((parent.shape[1], parent.shape[1]), f32)],
         compiler_params=pltpu.CompilerParams(vmem_limit_bytes=4 << 20),
         name="masks",
-    )(pos, parent, prefix)
+    )(pos, jnp.concatenate([parent, prefix], axis=0))
     keys = kv.shape[0]
     head = (pos, lim, reach)
     rest = [qg]
@@ -373,8 +335,8 @@
     trunk = swap(trunk, ("x", "z", "yl"))
     high = lax.div(yh, 2)
     part = q_keep + meet(q_send, "yh", 1).astype(f32)
-    query_grad = pick(part, high) + meet(pick(part, 1 - high).astype(bf16), "yh", 2).astype(f32)
-    query_grad = query_grad.astype(bf16)
+    rest = meet(pick(part, 1 - high).astype(bf16), "yh", 2)
+    query_grad = (pick(part, high) + rest.astype(f32)).astype(bf16)
     high = lax.div(x, 2)
     part = t_keep + meet(t_send, "x", 1)
     branch = pick(part, high) + meet(pick(part, 1 - high), "x", 2)

time: 95 us -> 95.2 us (level)
  Pallas kernels: 14.4 us -> 12.1 us
  other arithmetic: 4.02 us -> 5.62 us
  waiting for transfers between devices: 14.2 us -> 15.6 us
    pallas_call x1 -> x0, Pallas kernels: 2.45 us -> none  [per_device(): pl.pallas_call(pack_kernel, out_shape=(shape((ny, 2) + queries.shape[1:],...]
    unnamed x4 -> x0, local copies, waits for them, and re-layouts: 1.36 us -> none
  transfers between devices with their start and end apart: 10 -> 10, of which waited for: 4 -> 5; matrix products, arithmetic and copies ran while one was open for 4% -> 4% of each run, Pallas kernels for 5% -> 5%
where the time goes in v4:
time: 95.2 us; the launch traced here: 94.7 us
  starting transfers between devices  45.1 us (47%)
  waiting for transfers between devices  15.6 us (16%)
  blocking collectives  14.6 us (15%)
  Pallas kernels  12.1 us (13%)
  other arithmetic  5.62 us (6%)
    all_to_all x2, starting transfers between devices, swap(): return lax.all_to_all(x, axis, 0, 0)  20.3 us
    all_to_all x1, blocking collectives, swap(): return lax.all_to_all(x, axis, 0, 0)  14.6 us
    ppermute x4, starting transfers between devices, turn(): return lax.ppermute(x, axis, [(i, (i + k) % n) for i in range(n)])  12.4 us
    ppermute x4, starting transfers between devices, meet(): lax.ppermute(x, axis, [(i, i ^ bit) for i in range(lax.axis_size(axis))])  12.3 us
    ppermute x4, waiting for transfers between devices, meet(): lax.ppermute(x, axis, [(i, i ^ bit) for i in range(lax.axis_size(axis))])  6.94 us
    pallas_call x2, Pallas kernels, per_device(): pl.pallas_call(functools.partial(stats_kernel, shifts[half], half == 1),...  5.51 us
    all_to_all x2, waiting for transfers between devices, swap(): return lax.all_to_all(x, axis, 0, 0)  5.48 us
    pallas_call x1, Pallas kernels, per_device(): pl.pallas_call(functools.partial(grads_kernel, shifts), out_shape=(shape(...  4.29 us
  transfers between devices with their start and end apart: 10, of which 5 were waited for; matrix products, arithmetic and copies ran while one was open for 4% of the time, Pallas kernels for 5%

profile of v4, /device:TPU:2, one launch (start us, length us, event | category | flops | bytes accessed | tf_op | source)
XLA Modules:
  0.0 94.7 jit_solution(13596558013766324544)
XLA Ops:
  0.6 0.9 pad_maximum_fusion.1
  1.5 0.8 broadcast_in_dim.8
  2.4 7.1 %all-to-all-start = ((bf16[4,2,16,2048]{3,2,1,0:T(8,128)(2,1)}), bf16[4,2,16,2048]{3,2,1,0:T(8,128)(2,1)S(1)}, u32[]{:S(2)}, u32[]{:S(2)}) async-start(bf16[4,2,16,2048]{3,2,1,0:T(8,128)(2,1)} %broadcast_in_dim.8), calls=%async_computation | async-start | bytes 1048576 | tf_op jit(solution)/shard_map/all_to_all | solution.py:238
  9.5 1.0 %pad_maximum_fusion.refs_1_.refs_6_ = bf16[528,256]{1,0:T(8,128)(2,1)S(1)} fusion(bf16[16,256]{1,0:T(8,128)(2,1)} %bitcast.23, bf16[512,256]{1,0:T(8,128)(2,1)} %param.9), kind=kLoop, calls=%fused_computation.2 | loop fusion | flops 540672 | bytes 540672 | tf_op jit(solution)/shard_map/concatenate | solution.py:274
  10.5 3.4 %collective-permute-start = (bf16[528,256]{1,0:T(8,128)(2,1)S(1)}, bf16[528,256]{1,0:T(8,128)(2,1)S(1)}, u32[]{:S(2)}, u32[]{:S(2)}) collective-permute-start(bf16[528,256]{1,0:T(8,128)(2,1)S(1)} %pad_maximum_fusion.refs_1_.refs_6_), channel_id=1, source_target_pairs={{0,32},{32,64},{64,96},{96,0},{1,33},{33,65},{65,97},{97,1},{2,34}... | collective-permute-start | bytes 811016 | tf_op jit(solution)/shard_map/ppermute | solution.py:247
  13.9 4.8 %collective-permute-start.1 = (bf16[528,256]{1,0:T(8,128)(2,1)S(1)}, bf16[528,256]{1,0:T(8,128)(2,1)S(1)}, u32[]{:S(2)}, u32[]{:S(2)}) collective-permute-start(bf16[528,256]{1,0:T(8,128)(2,1)S(1)} %pad_maximum_fusion.refs_1_.refs_6_), channel_id=1, source_target_pairs={{0,64},{32,96},{64,0},{96,32},{1,65},{33,97},{65,1},{97,33},{2,66}... | collective-permute-start | bytes 811016 | tf_op jit(solution)/shard_map/ppermute | solution.py:247
  18.6 2.3 %collective-permute-start.2 = (bf16[528,256]{1,0:T(8,128)(2,1)S(1)}, bf16[528,256]{1,0:T(8,128)(2,1)S(1)}, u32[]{:S(2)}, u32[]{:S(2)}) collective-permute-start(bf16[528,256]{1,0:T(8,128)(2,1)S(1)} %pad_maximum_fusion.refs_1_.refs_6_), channel_id=1, source_target_pairs={{0,96},{32,0},{64,32},{96,64},{1,97},{33,1},{65,33},{97,65},{2,98}... | collective-permute-start | bytes 811016 | tf_op jit(solution)/shard_map/ppermute | solution.py:247
  21.0 0.1 pad_add_fusion.1.pos_ref
  21.0 0.7 pad_add_fusion.trees_ref
  21.7 2.3 %masks.1 = (s32[1,1024]{1,0:T(1,128)S(1)}, f32[64,1024]{1,0:T(8,128)S(1)}) custom-call(s32[3]{0:T(128)S(1)} %pad_add_fusion.1.pos_ref, s32[2,256]{1,0:T(2,128)S(1)} %pad_add_fusion.trees_ref), custom_call_target="tpu_custom_call" | custom-call | tf_op jit(solution)/shard_map/masks/pallas_call | solution.py:280
  24.1 0.0 collective-permute-done.refs_2_.refs_7_
  24.1 0.6 all-to-all-done.refs_0_
  24.7 2.8 %stats.2 = (f32[3,1024]{1,0:T(4,128)S(1)}, f32[2,1024]{1,0:T(2,128)S(1)}, f32[2,528,1024]{2,1,0:T(8,128)S(1)}, f32[2,528,1024]{2,1,0:T(8,128)S(1)}, bf16[1024,12...) custom-call(s32[3]{0:T(128)S(1)} %pad_add_fusion.1.pos_ref, s32[1,1024]{1,0:T(1,128)S(1)} %get-tuple-element.21.lim_ref, ...), custom_call_target="tpu_custom_call" | custom-call | tf_op jit(solution)/shard_map/stats/pallas_call | solution.py:303
  27.6 0.0 collective-permute-done.1.refs_3_.refs_8_
  27.6 3.1 %collective-permute-done.2.refs_4_.refs_9_ = bf16[528,256]{1,0:T(8,128)(2,1)S(1)} collective-permute-done((bf16[528,256]{1,0:T(8,128)(2,1)S(1)}, bf16[528,256]{1,0:T(8,128)(2,1)S(1)}, u32[]{:S(2)}, u32[]{:S(2)}) %collective-permute-start.2) | collective-permute-done | bytes 270368 | tf_op jit(solution)/shard_map/ppermute | solution.py:247
  30.7 2.7 %stats.3 = (f32[2,1024]{1,0:T(2,128)S(1)}, f32[2,1024]{1,0:T(2,128)S(1)}, f32[2,528,1024]{2,1,0:T(8,128)S(1)}, f32[2,528,1024]{2,1,0:T(8,128)S(1)}) custom-call(s32[3]{0:T(128)S(1)} %pad_add_fusion.1.pos_ref, s32[1,1024]{1,0:T(1,128)S(1)} %get-tuple-element.21.lim_ref, f32[64,1024]{1,0:T(8,128)S(1)} %get-tuple-element.22.reach_ref, ...), custom_call_target="tpu_custom_call" | custom-call | tf_op jit(solution)/shard_map/stats/pallas_call | solution.py:303
  33.4 14.6 %all_to_all.15.stats_ref = f32[4,2,1024]{2,1,0:T(2,128)S(1)} all-to-all(f32[4,2,1024]{2,1,0:T(2,128)S(1)} %broadcast_in_dim.9), channel_id=1, replica_groups=mesh['yh'=4,'x'=4,'z'=8,'yl'=2,'c'=2] {'yh'}, dimensions={0} | all-to-all | bytes 65536 | tf_op jit(solution)/shard_map/all_to_all | solution.py:238
  48.0 4.3 %grads.1 = (f32[2,16,2048]{2,1,0:T(8,128)S(1)}, bf16[2,16,2048]{2,1,0:T(8,128)(2,1)S(1)}, f32[4,16,16,256]{3,2,1,0:T(8,128)S(1)}, bf16[4,16,16,256]{3,2,1,0:T(8,...) custom-call(s32[3]{0:T(128)S(1)} %pad_add_fusion.1.pos_ref, f32[4,2,1024]{2,1,0:T(2,128)S(1)} %all_to_all.15.stats_ref, ...), custom_call_target="tpu_custom_call" | custom-call | tf_op jit(solution)/shard_map/grads/pallas_call | solution.py:317
  52.3 1.9 %collective-permute-start.7 = (bf16[4,16,16,256]{3,2,1,0:T(8,128)(2,1)S(1)}, bf16[4,16,16,256]{3,2,1,0:T(8,128)(2,1)S(1)}, u32[]{:S(2)}, u32[]{:S(2)}) collective-permute-start(bf16[4,16,16,256]{3,2,1,0:T(8,128)(2,1)S(1)} %get-tuple-element.38), channel_id=1, source_target_pairs={{0,1},{1,0},{2,3},{3,2},{4,5},{5,4},{6,7},{7,6},{8,9},{9,8},{10,11... | collective-permute-start | bytes 1572872 | tf_op jit(solution)/shard_map/ppermute | solution.py:247
  54.2 2.3 %collective-permute-start.5 = (f32[2,16,256]{2,1,0:T(8,128)S(1)}, f32[2,16,256]{2,1,0:T(8,128)S(1)}, u32[]{:S(2)}, u32[]{:S(2)}) collective-permute-start(f32[2,16,256]{2,1,0:T(8,128)S(1)} %get-tuple-element.36), channel_id=1, source_target_pairs={{0,32},{32,0},{64,96},{96,64},{1,33},{33,1},{65,97},{97,65},{2,34}... | collective-permute-start | bytes 98312 | tf_op jit(solution)/shard_map/ppermute | solution.py:251
  56.5 2.5 %collective-permute-start.3 = (bf16[2,16,2048]{2,1,0:T(8,128)(2,1)S(1)}, bf16[2,16,2048]{2,1,0:T(8,128)(2,1)S(1)}, u32[]{:S(2)}, u32[]{:S(2)}) collective-permute-start(bf16[2,16,2048]{2,1,0:T(8,128)(2,1)S(1)} %get-tuple-element.34), channel_id=1, source_target_pairs={{0,128},{128,0},{256,384},{384,256},{1,129},{129,1},{257,385},{385... | collective-permute-start | bytes 393224 | tf_op jit(solution)/shard_map/ppermute | solution.py:251
  59.0 1.0 %collective-permute-done.5 = f32[2,16,256]{2,1,0:T(8,128)S(1)} collective-permute-done((f32[2,16,256]{2,1,0:T(8,128)S(1)}, f32[2,16,256]{2,1,0:T(8,128)S(1)}, u32[]{:S(2)}, u32[]{:S(2)}) %collective-permute-start.5) | collective-permute-done | bytes 32800 | tf_op jit(solution)/shard_map/ppermute | solution.py:251
  60.0 3.8 %collective-permute-start.6 = (f32[16,256]{1,0:T(8,128)S(1)}, f32[16,256]{1,0:T(8,128)S(1)}, u32[]{:S(2)}, u32[]{:S(2)}) collective-permute-start(f32[16,256]{1,0:T(8,128)S(1)} %dynamic-slice_bitcast_fusion), channel_id=1, source_target_pairs={{0,64},{32,96},{64,0},{96,32},{1,65},{33,97},{65,1},{97,33},{2,66}... | collective-permute-start | bytes 49160 | tf_op jit(solution)/shard_map/ppermute | solution.py:251
  63.8 0.0 collective-permute-done.7
  63.8 1.0 %add_convert_fusion = bf16[4,16,16,256]{3,2,1,0:T(8,128)(2,1)} fusion(f32[4,16,16,256]{3,2,1,0:T(8,128)S(1)} %get-tuple-element.37, bf16[4,16,16,256]{3,2,1,0:T(8,128)(2,1)S(1)} %collective-permute-done.7), kind=kLoop, calls=%fused_computation.1 | loop fusion | flops 786432 | bytes 2097152 | tf_op jit(solution)/shard_map/convert_element_type | solution.py:334
  64.8 13.2 %all-to-all-start.2 = ((bf16[64,16,256]{2,1,0:T(8,128)(2,1)}), bf16[64,16,256]{2,1,0:T(8,128)(2,1)S(1)}, u32[]{:S(2)}, u32[]{:S(2)}) async-start(bf16[64,16,256]{2,1,0:T(8,128)(2,1)} %bitcast.10), calls=%async_computation.2 | async-start | bytes 1048576 | tf_op jit(solution)/shard_map/all_to_all | solution.py:238
  78.1 0.0 collective-permute-done.3
  78.1 3.8 %collective-permute-start.4 = (bf16[16,2048]{1,0:T(8,128)(2,1)S(1)}, bf16[16,2048]{1,0:T(8,128)(2,1)S(1)}, u32[]{:S(2)}, u32[]{:S(2)}) collective-permute-start(bf16[16,2048]{1,0:T(8,128)(2,1)S(1)} %fusion.1), channel_id=1, source_target_pairs={{0,256},{128,384},{256,0},{384,128},{1,257},{129,385},{257,1},{385... | collective-permute-start | bytes 196616 | tf_op jit(solution)/shard_map/ppermute | solution.py:251
  81.9 0.0 collective-permute-done.6
  81.9 0.6 fusion.3
  82.5 5.9 %collective-permute-done.4 = bf16[16,2048]{1,0:T(8,128)(2,1)S(1)} collective-permute-done((bf16[16,2048]{1,0:T(8,128)(2,1)S(1)}, bf16[16,2048]{1,0:T(8,128)(2,1)S(1)}, u32[]{:S(2)}, u32[]{:S(2)}) %collective-permute-start.4) | collective-permute-done | bytes 65568 | tf_op jit(solution)/shard_map/ppermute | solution.py:251
  88.5 0.6 fusion.2
  89.1 4.8 %all-to-all-done.2 = bf16[64,16,256]{2,1,0:T(8,128)(2,1)S(1)} async-done(((bf16[64,16,256]{2,1,0:T(8,128)(2,1)}), bf16[64,16,256]{2,1,0:T(8,128)(2,1)S(1)}, u32[]{:S(2)}, u32[]{:S(2)}) %all-to-all-start.2) | async-done | bytes 524320 | tf_op jit(solution)/shard_map/all_to_all | solution.py:238
  94.0 0.7 convert_reduce_fusion
  (5 shorter events, 0.1 us)
Async XLA Ops:
  2.4 22.4 %all-to-all-start = ((bf16[4,2,16,2048]{3,2,1,0:T(8,128)(2,1)}), bf16[4,2,16,2048]{3,2,1,0:T(8,128)(2,1)S(1)}, u32[]{:S(2)}, u32[]{:S(2)}) async-start(bf16[4,2,16,2048]{3,2,1,0:T(8,128)(2,1)} %broadcast_in_dim.8), calls=%async_computation | async-start | bytes 1048576 | tf_op jit(solution)/shard_map/all_to_all | solution.py:238
  10.5 13.6 %collective-permute-start = (bf16[528,256]{1,0:T(8,128)(2,1)S(1)}, bf16[528,256]{1,0:T(8,128)(2,1)S(1)}, u32[]{:S(2)}, u32[]{:S(2)}) collective-permute-start(bf16[528,256]{1,0:T(8,128)(2,1)S(1)} %pad_maximum_fusion.refs_1_.refs_6_), channel_id=1, source_target_pairs={{0,32},{32,64},{64,96},{96,0},{1,33},{33,65},{65,97},{97,1},{2,34}... | collective-permute-start | bytes 811016 | tf_op jit(solution)/shard_map/ppermute | solution.py:247
  13.9 13.7 %collective-permute-start.1 = (bf16[528,256]{1,0:T(8,128)(2,1)S(1)}, bf16[528,256]{1,0:T(8,128)(2,1)S(1)}, u32[]{:S(2)}, u32[]{:S(2)}) collective-permute-start(bf16[528,256]{1,0:T(8,128)(2,1)S(1)} %pad_maximum_fusion.refs_1_.refs_6_), channel_id=1, source_target_pairs={{0,64},{32,96},{64,0},{96,32},{1,65},{33,97},{65,1},{97,33},{2,66}... | collective-permute-start | bytes 811016 | tf_op jit(solution)/shard_map/ppermute | solution.py:247
  18.6 12.1 %collective-permute-start.2 = (bf16[528,256]{1,0:T(8,128)(2,1)S(1)}, bf16[528,256]{1,0:T(8,128)(2,1)S(1)}, u32[]{:S(2)}, u32[]{:S(2)}) collective-permute-start(bf16[528,256]{1,0:T(8,128)(2,1)S(1)} %pad_maximum_fusion.refs_1_.refs_6_), channel_id=1, source_target_pairs={{0,96},{32,0},{64,32},{96,64},{1,97},{33,1},{65,33},{97,65},{2,98}... | collective-permute-start | bytes 811016 | tf_op jit(solution)/shard_map/ppermute | solution.py:247
  52.3 11.5 %collective-permute-start.7 = (bf16[4,16,16,256]{3,2,1,0:T(8,128)(2,1)S(1)}, bf16[4,16,16,256]{3,2,1,0:T(8,128)(2,1)S(1)}, u32[]{:S(2)}, u32[]{:S(2)}) collective-permute-start(bf16[4,16,16,256]{3,2,1,0:T(8,128)(2,1)S(1)} %get-tuple-element.38), channel_id=1, source_target_pairs={{0,1},{1,0},{2,3},{3,2},{4,5},{5,4},{6,7},{7,6},{8,9},{9,8},{10,11... | collective-permute-start | bytes 1572872 | tf_op jit(solution)/shard_map/ppermute | solution.py:247
  54.2 5.8 %collective-permute-start.5 = (f32[2,16,256]{2,1,0:T(8,128)S(1)}, f32[2,16,256]{2,1,0:T(8,128)S(1)}, u32[]{:S(2)}, u32[]{:S(2)}) collective-permute-start(f32[2,16,256]{2,1,0:T(8,128)S(1)} %get-tuple-element.36), channel_id=1, source_target_pairs={{0,32},{32,0},{64,96},{96,64},{1,33},{33,1},{65,97},{97,65},{2,34}... | collective-permute-start | bytes 98312 | tf_op jit(solution)/shard_map/ppermute | solution.py:251
  56.5 21.5 %collective-permute-start.3 = (bf16[2,16,2048]{2,1,0:T(8,128)(2,1)S(1)}, bf16[2,16,2048]{2,1,0:T(8,128)(2,1)S(1)}, u32[]{:S(2)}, u32[]{:S(2)}) collective-permute-start(bf16[2,16,2048]{2,1,0:T(8,128)(2,1)S(1)} %get-tuple-element.34), channel_id=1, source_target_pairs={{0,128},{128,0},{256,384},{384,256},{1,129},{129,1},{257,385},{385... | collective-permute-start | bytes 393224 | tf_op jit(solution)/shard_map/ppermute | solution.py:251
  60.0 21.9 %collective-permute-start.6 = (f32[16,256]{1,0:T(8,128)S(1)}, f32[16,256]{1,0:T(8,128)S(1)}, u32[]{:S(2)}, u32[]{:S(2)}) collective-permute-start(f32[16,256]{1,0:T(8,128)S(1)} %dynamic-slice_bitcast_fusion), channel_id=1, source_target_pairs={{0,64},{32,96},{64,0},{96,32},{1,65},{33,97},{65,1},{97,33},{2,66}... | collective-permute-start | bytes 49160 | tf_op jit(solution)/shard_map/ppermute | solution.py:251
  64.8 29.2 %all-to-all-start.2 = ((bf16[64,16,256]{2,1,0:T(8,128)(2,1)}), bf16[64,16,256]{2,1,0:T(8,128)(2,1)S(1)}, u32[]{:S(2)}, u32[]{:S(2)}) async-start(bf16[64,16,256]{2,1,0:T(8,128)(2,1)} %bitcast.10), calls=%async_computation.2 | async-start | bytes 1048576 | tf_op jit(solution)/shard_map/all_to_all | solution.py:238
  78.1 10.3 %collective-permute-start.4 = (bf16[16,2048]{1,0:T(8,128)(2,1)S(1)}, bf16[16,2048]{1,0:T(8,128)(2,1)S(1)}, u32[]{:S(2)}, u32[]{:S(2)}) collective-permute-start(bf16[16,2048]{1,0:T(8,128)(2,1)S(1)} %fusion.1), channel_id=1, source_target_pairs={{0,256},{128,384},{256,0},{384,128},{1,257},{129,385},{257,1},{385... | collective-permute-start | bytes 196616 | tf_op jit(solution)/shard_map/ppermute | solution.py:251

commit v5 on v4

--- a/solution.py
+++ b/solution.py
@@ -68,9 +68,9 @@
     lim_ref[...] = lim - yh * span
 
 
-def stats_kernel(shifts, last, pos_ref, lim_ref, reach_ref, *refs):
+def stats_kernel(shifts, first, last, pos_ref, lim_ref, reach_ref, *refs):
     count = len(shifts)
-    if last:
+    if not first:
         qs, gs, before_ref = refs[:3]
         kvs = refs[3 : 3 + count]
         after_ref, tops_ref, e_ref, s_ref = refs[3 + count :]
@@ -87,7 +87,7 @@
     trunk = keys - TILE
     power = scale * math.log2(math.e)
     ids = lax.broadcasted_iota(jnp.int32, (trunk, lanes), 0)
-    if last:
+    if not first:
         top, total, slope = (before_ref[i : i + 1, :] for i in range(3))
     else:
         top = jnp.full((1, lanes), MASKED, jnp.float32)
@@ -142,15 +142,17 @@
 
 
 def grads_kernel(shifts, pos_ref, stats_ref, qs, gs, *refs):
-    blocks = len(shifts[0]) + len(shifts[1])
-    kvs = refs[6 : 6 + blocks]
+    calls = len(shifts)
+    blocks = sum(map(len, shifts))
+    kvs = refs[3 * calls : 3 * calls + blocks]
+    refs = refs[:3 * calls] + refs[3 * calls + blocks :]
     held = [
         (k, kvs[k], refs[3 * half].at[pl.ds(i, 1)], refs[3 * half + 1].at[i], refs[3 * half + 2].at[i])
-        for half in range(2)
+        for half in range(calls)
         for i, k in enumerate(shifts[half])
     ]
-    qkeep_ref, qsend_ref, keep_ref, send_ref, tkeep_ref, tsend_ref = refs[6 + blocks : 12 + blocks]
-    d_scr, p_scr, tree_d, tree_k, kv_scr, tree_scr, dq_scr, q_scr = refs[12 + blocks :]
+    qkeep_ref, qsend_ref, keep_ref, send_ref, tkeep_ref, tsend_ref = refs[3 * calls :][:6]
+    d_scr, p_scr, tree_d, tree_k, kv_scr, tree_scr, dq_scr, q_scr = refs[3 * calls + 6 :]
     _, keys, lanes = d_scr.shape
     groups = stats_ref.shape[0]
     own = qkeep_ref.shape[1]
@@ -275,7 +277,7 @@
     kvs = [kv] + [None] * (nx - 1)
     for k in range(1, nx):
         kvs[k] = turn(kv, "x", k)
-    shifts = ((0, 1), (2, 3))
+    shifts = ((0, 2), (1,), (3,))
 
     lim, reach = pl.pallas_call(
         functools.partial(masks_kernel, nx, own, span),
@@ -290,18 +292,19 @@
     head = (pos, lim, reach)
     rest = [qg]
     held = []
-    for half in range(2):
+    for half in range(len(shifts)):
+        first, last = half == 0, half == len(shifts) - 1
         count = len(shifts[half])
         outs = [
-            shape((3 - half, lanes), f32),
+            shape((2 if last else 3, lanes), f32),
             shape((count, lanes), f32),
             shape((count, keys, lanes), f32),
             shape((count, keys, lanes), f32),
         ]
-        if half == 0:
+        if first:
             outs += [shape((lanes, width), bf16)] * 2
         stats, tops, e, s, *stacked = pl.pallas_call(
-            functools.partial(stats_kernel, shifts[half], half == 1),
+            functools.partial(stats_kernel, shifts[half], first, last),
             out_shape=tuple(outs),
             in_specs=[smem] + [vmem] * (2 + len(rest) + count),
             out_specs=(vmem,) * len(outs),
@@ -309,9 +312,9 @@
             name="stats",
         )(*head, *rest, *[kvs[k] for k in shifts[half]])
         held += [tops, e, s]
-        if half == 0:
+        if first:
             qs, gs = stacked
-            rest = [qs, gs, stats]
+        rest = [qs, gs, stats]
     stats = spread(stats, "yh")
     pieces = trunk_kv.shape[0] // (2 * own)
     q_keep, q_send, keep, send, t_keep, t_send = pl.pallas_call(
@@ -324,7 +327,7 @@
             shape((nx // 2, own, 2 * width), f32),
             shape((nx // 2, own, 2 * width), f32),
         ),
-        in_specs=[smem] + [vmem] * (9 + nx),
+        in_specs=[smem] + [vmem] * (3 + len(held) + nx),
         out_specs=(vmem,) * 6,
         scratch_shapes=grads_scratch(keys, lanes, width, nx, ny, own),
         compiler_params=pltpu.CompilerParams(vmem_limit_bytes=12 << 20),

time: 95.2 us -> 93 us (0.977)
  waiting for transfers between devices: 15.6 us -> 12.9 us
    ppermute x4, waiting for transfers between devices: 3.14 us -> 0.09 us  [turn(): return lax.ppermute(x, axis, [(i, (i + k) % n) for i in range(n)])]
    all_to_all x2, waiting for transfers between devices: 5.48 us -> 6.89 us  [swap(): return lax.all_to_all(x, axis, 0, 0)]
    ppermute x4, waiting for transfers between devices: 6.94 us -> 5.92 us  [meet(): lax.ppermute(x, axis, [(i, i ^ bit) for i in range(lax.axis_size(axis))])]
    pallas_call x2 -> x3, Pallas kernels: 5.51 us -> 6.22 us  [per_device(): pl.pallas_call(functools.partial(stats_kernel, shifts[half], first, last)...]
  transfers between devices with their start and end apart: 10 -> 10, of which waited for: 5 -> 5; matrix products, arithmetic and copies ran while one was open for 4% -> 4% of each run, Pallas kernels for 5% -> 7%
where the time goes in v5:
time: 93 us; the launch traced here: 92.4 us
  starting transfers between devices  45.4 us (49%)
  blocking collectives  14.6 us (16%)
  waiting for transfers between devices  12.9 us (14%)
  Pallas kernels  12.8 us (14%)
  other arithmetic  4.94 us (5%)
    all_to_all x2, starting transfers between devices, swap(): return lax.all_to_all(x, axis, 0, 0)  20.7 us
    all_to_all x1, blocking collectives, swap(): return lax.all_to_all(x, axis, 0, 0)  14.6 us
    ppermute x4, starting transfers between devices, meet(): lax.ppermute(x, axis, [(i, i ^ bit) for i in range(lax.axis_size(axis))])  13 us
    ppermute x4, starting transfers between devices, turn(): return lax.ppermute(x, axis, [(i, (i + k) % n) for i in range(n)])  11.8 us
    all_to_all x2, waiting for transfers between devices, swap(): return lax.all_to_all(x, axis, 0, 0)  6.89 us
    pallas_call x3, Pallas kernels, per_device(): pl.pallas_call(functools.partial(stats_kernel, shifts[half], first, last)...  6.22 us
    ppermute x4, waiting for transfers between devices, meet(): lax.ppermute(x, axis, [(i, i ^ bit) for i in range(lax.axis_size(axis))])  5.92 us
    pallas_call x1, Pallas kernels, per_device(): pl.pallas_call(functools.partial(grads_kernel, shifts), out_shape=(shape(...  4.29 us
  transfers between devices with their start and end apart: 10, of which 5 were waited for; matrix products, arithmetic and copies ran while one was open for 4% of the time, Pallas kernels for 7%

profile of v5, /device:TPU:2, one launch (start us, length us, event | category | flops | bytes accessed | tf_op | source)
XLA Modules:
  0.0 92.4 jit_solution(15742838384248220196)
XLA Ops:
  0.6 0.0 copy-start.1
  0.6 0.0 copy-start
  0.7 0.9 pad_maximum_fusion.1
  1.6 0.8 broadcast_in_dim.8
  2.4 7.1 %all-to-all-start = ((bf16[4,2,16,2048]{3,2,1,0:T(8,128)(2,1)}), bf16[4,2,16,2048]{3,2,1,0:T(8,128)(2,1)S(1)}, u32[]{:S(2)}, u32[]{:S(2)}) async-start(bf16[4,2,16,2048]{3,2,1,0:T(8,128)(2,1)} %broadcast_in_dim.8), calls=%async_computation | async-start | bytes 1048576 | tf_op jit(solution)/shard_map/all_to_all | solution.py:240
  9.5 1.0 %pad_maximum_fusion.refs_1_.refs_9_ = bf16[528,256]{1,0:T(8,128)(2,1)S(1)} fusion(bf16[16,256]{1,0:T(8,128)(2,1)} %bitcast.23, bf16[512,256]{1,0:T(8,128)(2,1)} %param.9), kind=kLoop, calls=%fused_computation.2 | loop fusion | flops 540672 | bytes 540672 | tf_op jit(solution)/shard_map/concatenate | solution.py:276
  10.5 4.0 %collective-permute-start = (bf16[528,256]{1,0:T(8,128)(2,1)S(1)}, bf16[528,256]{1,0:T(8,128)(2,1)S(1)}, u32[]{:S(2)}, u32[]{:S(2)}) collective-permute-start(bf16[528,256]{1,0:T(8,128)(2,1)S(1)} %pad_maximum_fusion.refs_1_.refs_9_), channel_id=1, source_target_pairs={{0,64},{32,96},{64,0},{96,32},{1,65},{33,97},{65,1},{97,33},{2,66}... | collective-permute-start | bytes 811016 | tf_op jit(solution)/shard_map/ppermute | solution.py:249
  14.5 3.5 %collective-permute-start.1 = (bf16[528,256]{1,0:T(8,128)(2,1)S(1)}, bf16[528,256]{1,0:T(8,128)(2,1)S(1)}, u32[]{:S(2)}, u32[]{:S(2)}) collective-permute-start(bf16[528,256]{1,0:T(8,128)(2,1)S(1)} %pad_maximum_fusion.refs_1_.refs_9_), channel_id=1, source_target_pairs={{0,32},{32,64},{64,96},{96,0},{1,33},{33,65},{65,97},{97,1},{2,34}... | collective-permute-start | bytes 811016 | tf_op jit(solution)/shard_map/ppermute | solution.py:249
  18.0 2.3 %collective-permute-start.2 = (bf16[528,256]{1,0:T(8,128)(2,1)S(1)}, bf16[528,256]{1,0:T(8,128)(2,1)S(1)}, u32[]{:S(2)}, u32[]{:S(2)}) collective-permute-start(bf16[528,256]{1,0:T(8,128)(2,1)S(1)} %pad_maximum_fusion.refs_1_.refs_9_), channel_id=1, source_target_pairs={{0,96},{32,0},{64,32},{96,64},{1,97},{33,1},{65,33},{97,65},{2,98}... | collective-permute-start | bytes 811016 | tf_op jit(solution)/shard_map/ppermute | solution.py:249
  20.4 0.1 pad_add_fusion.1.pos_ref
  20.5 0.0 copy-done.1
  20.5 0.0 copy-done
  20.5 2.3 %masks.1 = (s32[1,1024]{1,0:T(1,128)S(1)}, f32[64,1024]{1,0:T(8,128)S(1)}) custom-call(s32[3]{0:T(128)S(1)} %pad_add_fusion.1.pos_ref, s32[2,256]{1,0:T(2,128)S(1)} %pad_add_fusion.trees_ref), custom_call_target="tpu_custom_call" | custom-call | tf_op jit(solution)/shard_map/masks/pallas_call | solution.py:282
  22.8 0.0 collective-permute-done.refs_2_.refs_11_
  22.8 1.9 %all-to-all-done.refs_0_ = bf16[4,2,16,2048]{3,2,1,0:T(8,128)(2,1)S(1)} async-done(((bf16[4,2,16,2048]{3,2,1,0:T(8,128)(2,1)}), bf16[4,2,16,2048]{3,2,1,0:T(8,128)(2,1)S(1)}, u32[]{:S(2)}, u32[]{:S(2)}) %all-to-all-start) | async-done | bytes 524320 | tf_op jit(solution)/shard_map/all_to_all | solution.py:240
  24.8 2.8 %stats.3 = (f32[3,1024]{1,0:T(4,128)S(1)}, f32[2,1024]{1,0:T(2,128)S(1)}, f32[2,528,1024]{2,1,0:T(8,128)S(1)}, f32[2,528,1024]{2,1,0:T(8,128)S(1)}, bf16[1024,12...) custom-call(s32[3]{0:T(128)S(1)} %pad_add_fusion.1.pos_ref, s32[1,1024]{1,0:T(1,128)S(1)} %get-tuple-element.25.lim_ref, ...), custom_call_target="tpu_custom_call" | custom-call | tf_op jit(solution)/shard_map/stats/pallas_call | solution.py:306
  27.6 0.1 collective-permute-done.1.refs_3_.refs_10_
  27.7 1.7 %stats.4 = (f32[3,1024]{1,0:T(4,128)S(1)}, f32[1,1024]{1,0:T(1,128)S(1)}, f32[1,528,1024]{2,1,0:T(8,128)S(1)}, f32[1,528,1024]{2,1,0:T(8,128)S(1)}) custom-call(s32[3]{0:T(128)S(1)} %pad_add_fusion.1.pos_ref, s32[1,1024]{1,0:T(1,128)S(1)} %get-tuple-element.25.lim_ref, f32[64,1024]{1,0:T(8,128)S(1)} %get-tuple-element.26.reach_ref, ...), custom_call_target="tpu_custom_call" | custom-call | tf_op jit(solution)/shard_map/stats/pallas_call | solution.py:306
  29.4 0.0 collective-permute-done.2.refs_3_.refs_12_
  29.4 1.7 %stats.5 = (f32[2,1024]{1,0:T(2,128)S(1)}, f32[1,1024]{1,0:T(1,128)S(1)}, f32[1,528,1024]{2,1,0:T(8,128)S(1)}, f32[1,528,1024]{2,1,0:T(8,128)S(1)}) custom-call(s32[3]{0:T(128)S(1)} %pad_add_fusion.1.pos_ref, s32[1,1024]{1,0:T(1,128)S(1)} %get-tuple-element.25.lim_ref, f32[64,1024]{1,0:T(8,128)S(1)} %get-tuple-element.26.reach_ref, ...), custom_call_target="tpu_custom_call" | custom-call | tf_op jit(solution)/shard_map/stats/pallas_call | solution.py:306
  31.1 14.6 %all_to_all.15.stats_ref = f32[4,2,1024]{2,1,0:T(2,128)S(1)} all-to-all(f32[4,2,1024]{2,1,0:T(2,128)S(1)} %broadcast_in_dim.9), channel_id=1, replica_groups=mesh['yh'=4,'x'=4,'z'=8,'yl'=2,'c'=2] {'yh'}, dimensions={0} | all-to-all | bytes 65536 | tf_op jit(solution)/shard_map/all_to_all | solution.py:240
  45.7 4.3 %grads.1 = (f32[2,16,2048]{2,1,0:T(8,128)S(1)}, bf16[2,16,2048]{2,1,0:T(8,128)(2,1)S(1)}, f32[4,16,16,256]{3,2,1,0:T(8,128)S(1)}, bf16[4,16,16,256]{3,2,1,0:T(8,...) custom-call(s32[3]{0:T(128)S(1)} %pad_add_fusion.1.pos_ref, f32[4,2,1024]{2,1,0:T(2,128)S(1)} %all_to_all.15.stats_ref, ...), custom_call_target="tpu_custom_call" | custom-call | tf_op jit(solution)/shard_map/grads/pallas_call | solution.py:320
  50.0 1.9 %collective-permute-start.7 = (bf16[4,16,16,256]{3,2,1,0:T(8,128)(2,1)S(1)}, bf16[4,16,16,256]{3,2,1,0:T(8,128)(2,1)S(1)}, u32[]{:S(2)}, u32[]{:S(2)}) collective-permute-start(bf16[4,16,16,256]{3,2,1,0:T(8,128)(2,1)S(1)} %get-tuple-element.46), channel_id=1, source_target_pairs={{0,1},{1,0},{2,3},{3,2},{4,5},{5,4},{6,7},{7,6},{8,9},{9,8},{10,11... | collective-permute-start | bytes 1572872 | tf_op jit(solution)/shard_map/ppermute | solution.py:249
  51.9 3.2 %collective-permute-start.5 = (f32[2,16,256]{2,1,0:T(8,128)S(1)}, f32[2,16,256]{2,1,0:T(8,128)S(1)}, u32[]{:S(2)}, u32[]{:S(2)}) collective-permute-start(f32[2,16,256]{2,1,0:T(8,128)S(1)} %get-tuple-element.44), channel_id=1, source_target_pairs={{0,32},{32,0},{64,96},{96,64},{1,33},{33,1},{65,97},{97,65},{2,34}... | collective-permute-start | bytes 98312 | tf_op jit(solution)/shard_map/ppermute | solution.py:253
  55.1 2.5 %collective-permute-start.3 = (bf16[2,16,2048]{2,1,0:T(8,128)(2,1)S(1)}, bf16[2,16,2048]{2,1,0:T(8,128)(2,1)S(1)}, u32[]{:S(2)}, u32[]{:S(2)}) collective-permute-start(bf16[2,16,2048]{2,1,0:T(8,128)(2,1)S(1)} %get-tuple-element.42), channel_id=1, source_target_pairs={{0,128},{128,0},{256,384},{384,256},{1,129},{129,1},{257,385},{385... | collective-permute-start | bytes 393224 | tf_op jit(solution)/shard_map/ppermute | solution.py:253
  57.6 0.1 collective-permute-done.5
  57.7 3.4 %collective-permute-start.6 = (f32[16,256]{1,0:T(8,128)S(1)}, f32[16,256]{1,0:T(8,128)S(1)}, u32[]{:S(2)}, u32[]{:S(2)}) collective-permute-start(f32[16,256]{1,0:T(8,128)S(1)} %dynamic-slice_bitcast_fusion), channel_id=1, source_target_pairs={{0,64},{32,96},{64,0},{96,32},{1,65},{33,97},{65,1},{97,33},{2,66}... | collective-permute-start | bytes 49160 | tf_op jit(solution)/shard_map/ppermute | solution.py:253
  61.2 0.0 collective-permute-done.7
  61.2 1.0 %add_convert_fusion = bf16[4,16,16,256]{3,2,1,0:T(8,128)(2,1)} fusion(f32[4,16,16,256]{3,2,1,0:T(8,128)S(1)} %get-tuple-element.45, bf16[4,16,16,256]{3,2,1,0:T(8,128)(2,1)S(1)} %collective-permute-done.7), kind=kLoop, calls=%fused_computation.1 | loop fusion | flops 786432 | bytes 2097152 | tf_op jit(solution)/shard_map/convert_element_type | solution.py:337
  62.1 13.6 %all-to-all-start.2 = ((bf16[64,16,256]{2,1,0:T(8,128)(2,1)}), bf16[64,16,256]{2,1,0:T(8,128)(2,1)S(1)}, u32[]{:S(2)}, u32[]{:S(2)}) async-start(bf16[64,16,256]{2,1,0:T(8,128)(2,1)} %bitcast.10), calls=%async_computation.2 | async-start | bytes 1048576 | tf_op jit(solution)/shard_map/all_to_all | solution.py:240
  75.7 0.0 collective-permute-done.3
  75.8 3.9 %collective-permute-start.4 = (bf16[16,2048]{1,0:T(8,128)(2,1)S(1)}, bf16[16,2048]{1,0:T(8,128)(2,1)S(1)}, u32[]{:S(2)}, u32[]{:S(2)}) collective-permute-start(bf16[16,2048]{1,0:T(8,128)(2,1)S(1)} %fusion.1), channel_id=1, source_target_pairs={{0,256},{128,384},{256,0},{384,128},{1,257},{129,385},{257,1},{385... | collective-permute-start | bytes 196616 | tf_op jit(solution)/shard_map/ppermute | solution.py:253
  79.7 0.0 collective-permute-done.6
  79.7 0.6 fusion.3
  80.3 5.8 %collective-permute-done.4 = bf16[16,2048]{1,0:T(8,128)(2,1)S(1)} collective-permute-done((bf16[16,2048]{1,0:T(8,128)(2,1)S(1)}, bf16[16,2048]{1,0:T(8,128)(2,1)S(1)}, u32[]{:S(2)}, u32[]{:S(2)}) %collective-permute-start.4) | collective-permute-done | bytes 65568 | tf_op jit(solution)/shard_map/ppermute | solution.py:253
  86.1 0.6 fusion.2
  86.8 5.0 %all-to-all-done.2 = bf16[64,16,256]{2,1,0:T(8,128)(2,1)S(1)} async-done(((bf16[64,16,256]{2,1,0:T(8,128)(2,1)}), bf16[64,16,256]{2,1,0:T(8,128)(2,1)S(1)}, u32[]{:S(2)}, u32[]{:S(2)}) %all-to-all-start.2) | async-done | bytes 524320 | tf_op jit(solution)/shard_map/all_to_all | solution.py:240
  91.7 0.7 convert_reduce_fusion
  (6 shorter events, 0.1 us)
Async XLA Ops:
  0.6 19.8 %copy-start.1 = (s32[1,256]{1,0:T(1,128)S(1)}, s32[1,256]{1,0:T(1,128)}, u32[]{:S(2)}) copy-start(s32[1,256]{1,0:T(1,128)} %param.10) | copy-start | bytes 3076
  0.6 19.8 %copy-start = (s32[1,256]{1,0:T(1,128)S(1)}, s32[1,256]{1,0:T(1,128)}, u32[]{:S(2)}) copy-start(s32[1,256]{1,0:T(1,128)} %param.11) | copy-start | bytes 3076
  2.4 22.4 %all-to-all-start = ((bf16[4,2,16,2048]{3,2,1,0:T(8,128)(2,1)}), bf16[4,2,16,2048]{3,2,1,0:T(8,128)(2,1)S(1)}, u32[]{:S(2)}, u32[]{:S(2)}) async-start(bf16[4,2,16,2048]{3,2,1,0:T(8,128)(2,1)} %broadcast_in_dim.8), calls=%async_computation | async-start | bytes 1048576 | tf_op jit(solution)/shard_map/all_to_all | solution.py:240
  10.5 12.3 %collective-permute-start = (bf16[528,256]{1,0:T(8,128)(2,1)S(1)}, bf16[528,256]{1,0:T(8,128)(2,1)S(1)}, u32[]{:S(2)}, u32[]{:S(2)}) collective-permute-start(bf16[528,256]{1,0:T(8,128)(2,1)S(1)} %pad_maximum_fusion.refs_1_.refs_9_), channel_id=1, source_target_pairs={{0,64},{32,96},{64,0},{96,32},{1,65},{33,97},{65,1},{97,33},{2,66}... | collective-permute-start | bytes 811016 | tf_op jit(solution)/shard_map/ppermute | solution.py:249
  14.5 13.2 %collective-permute-start.1 = (bf16[528,256]{1,0:T(8,128)(2,1)S(1)}, bf16[528,256]{1,0:T(8,128)(2,1)S(1)}, u32[]{:S(2)}, u32[]{:S(2)}) collective-permute-start(bf16[528,256]{1,0:T(8,128)(2,1)S(1)} %pad_maximum_fusion.refs_1_.refs_9_), channel_id=1, source_target_pairs={{0,32},{32,64},{64,96},{96,0},{1,33},{33,65},{65,97},{97,1},{2,34}... | collective-permute-start | bytes 811016 | tf_op jit(solution)/shard_map/ppermute | solution.py:249
  18.0 11.3 %collective-permute-start.2 = (bf16[528,256]{1,0:T(8,128)(2,1)S(1)}, bf16[528,256]{1,0:T(8,128)(2,1)S(1)}, u32[]{:S(2)}, u32[]{:S(2)}) collective-permute-start(bf16[528,256]{1,0:T(8,128)(2,1)S(1)} %pad_maximum_fusion.refs_1_.refs_9_), channel_id=1, source_target_pairs={{0,96},{32,0},{64,32},{96,64},{1,97},{33,1},{65,33},{97,65},{2,98}... | collective-permute-start | bytes 811016 | tf_op jit(solution)/shard_map/ppermute | solution.py:249
  50.0 11.2 %collective-permute-start.7 = (bf16[4,16,16,256]{3,2,1,0:T(8,128)(2,1)S(1)}, bf16[4,16,16,256]{3,2,1,0:T(8,128)(2,1)S(1)}, u32[]{:S(2)}, u32[]{:S(2)}) collective-permute-start(bf16[4,16,16,256]{3,2,1,0:T(8,128)(2,1)S(1)} %get-tuple-element.46), channel_id=1, source_target_pairs={{0,1},{1,0},{2,3},{3,2},{4,5},{5,4},{6,7},{7,6},{8,9},{9,8},{10,11... | collective-permute-start | bytes 1572872 | tf_op jit(solution)/shard_map/ppermute | solution.py:249
  51.9 5.8 %collective-permute-start.5 = (f32[2,16,256]{2,1,0:T(8,128)S(1)}, f32[2,16,256]{2,1,0:T(8,128)S(1)}, u32[]{:S(2)}, u32[]{:S(2)}) collective-permute-start(f32[2,16,256]{2,1,0:T(8,128)S(1)} %get-tuple-element.44), channel_id=1, source_target_pairs={{0,32},{32,0},{64,96},{96,64},{1,33},{33,1},{65,97},{97,65},{2,34}... | collective-permute-start | bytes 98312 | tf_op jit(solution)/shard_map/ppermute | solution.py:253
  55.1 20.6 %collective-permute-start.3 = (bf16[2,16,2048]{2,1,0:T(8,128)(2,1)S(1)}, bf16[2,16,2048]{2,1,0:T(8,128)(2,1)S(1)}, u32[]{:S(2)}, u32[]{:S(2)}) collective-permute-start(bf16[2,16,2048]{2,1,0:T(8,128)(2,1)S(1)} %get-tuple-element.42), channel_id=1, source_target_pairs={{0,128},{128,0},{256,384},{384,256},{1,129},{129,1},{257,385},{385... | collective-permute-start | bytes 393224 | tf_op jit(solution)/shard_map/ppermute | solution.py:253
  57.7 22.0 %collective-permute-start.6 = (f32[16,256]{1,0:T(8,128)S(1)}, f32[16,256]{1,0:T(8,128)S(1)}, u32[]{:S(2)}, u32[]{:S(2)}) collective-permute-start(f32[16,256]{1,0:T(8,128)S(1)} %dynamic-slice_bitcast_fusion), channel_id=1, source_target_pairs={{0,64},{32,96},{64,0},{96,32},{1,65},{33,97},{65,1},{97,33},{2,66}... | collective-permute-start | bytes 49160 | tf_op jit(solution)/shard_map/ppermute | solution.py:253
  62.1 29.6 %all-to-all-start.2 = ((bf16[64,16,256]{2,1,0:T(8,128)(2,1)}), bf16[64,16,256]{2,1,0:T(8,128)(2,1)S(1)}, u32[]{:S(2)}, u32[]{:S(2)}) async-start(bf16[64,16,256]{2,1,0:T(8,128)(2,1)} %bitcast.10), calls=%async_computation.2 | async-start | bytes 1048576 | tf_op jit(solution)/shard_map/all_to_all | solution.py:240
  75.8 10.3 %collective-permute-start.4 = (bf16[16,2048]{1,0:T(8,128)(2,1)S(1)}, bf16[16,2048]{1,0:T(8,128)(2,1)S(1)}, u32[]{:S(2)}, u32[]{:S(2)}) collective-permute-start(bf16[16,2048]{1,0:T(8,128)(2,1)S(1)} %fusion.1), channel_id=1, source_target_pairs={{0,256},{128,384},{256,0},{384,128},{1,257},{129,385},{257,1},{385... | collective-permute-start | bytes 196616 | tf_op jit(solution)/shard_map/ppermute | solution.py:253
